TPU v7x, 32 devices: a whole 2x2x4 slice. The times are simulated.
32 devices in a mesh: expert: 8 (over z, core), cuts: 4 (over y, x).
Axes of the slice: x: 2, y: 2, z: 4, core: 2. Of those that a mesh axis runs over, the one named last changes fastest.
Arguments:
- block_input: bfloat16 [8192, 1024], P(('expert', 'cuts')), may hold values from -6 to 6
- routes: int32 [8192], P(('expert', 'cuts')), may hold values from 0 to 31, as said below
- kept_mask: int32 [8192], P(('expert', 'cuts')), may hold values from 0 to 1, as said below
- w_qkv: bfloat16 [1024, 3072], P('cuts'), may hold values from -0.1875 to 0.1875
- w_attn_out: bfloat16 [1024, 1024], P('cuts'), may hold values from -1 to 1
- w_in: bfloat16 [1024, 4096], P('cuts'), may hold values from -0.1875 to 0.1875
- w_out: bfloat16 [4096, 1024], P('cuts'), may hold values from -0.1875 to 0.1875
- w_router: bfloat16 [1024, 32], P('cuts'), may hold values from -0.09375 to 0.09375
- w_mix: bfloat16 [1024, 2], P('cuts'), may hold values from -0.1875 to 0.1875
- gain_attn: bfloat16 [1024], P('cuts'), may hold values from 0.5 to 1.5
- gain_ffn: bfloat16 [1024], P('cuts'), may hold values from 0.5 to 1.5
- expert_in: bfloat16 [32, 1024, 4096], P('expert', None, 'cuts'), may hold values from -0.1875 to 0.1875
- expert_out: bfloat16 [32, 4096, 1024], P('expert', 'cuts'), may hold values from -6 to 6
- cotangent: bfloat16 [8192, 1024], P(('expert', 'cuts')), may hold values from -6 to 6
Outputs:
- block_out: bfloat16 [8192, 1024], P(('expert', 'cuts'))
- d_block_input: float32 [8192, 1024], P(('expert', 'cuts'))
- d_w_qkv: float32 [1024, 3072], P(('expert', 'cuts'))
- d_w_attn_out: float32 [1024, 1024], P(('expert', 'cuts'))
- d_w_in: float32 [1024, 4096], P(('expert', 'cuts'))
- d_w_out: float32 [4096, 1024], P(('expert', 'cuts'))
- d_w_router: float32 [1024, 32], P(('expert', 'cuts'))
- d_w_mix: float32 [1024, 2], P(('expert', 'cuts'))
- d_gain_attn: float32 [1024], P(('expert', 'cuts'))
- d_gain_ffn: float32 [1024], P(('expert', 'cuts'))
- d_expert_in: float32 [32, 1024, 4096], P('expert', None, 'cuts')
- d_expert_out: float32 [32, 4096, 1024], P('expert', 'cuts')
Inputs may be any that keep to these rules, and one draw needn't show every extreme that they name: `routes`: the expert of each token; a few experts are far more common than the rest. kept_mask is 1 exactly for the first 12 tokens of each expert within the rows of one device, in token order; on every device some expert fills all 12 of its slots.
All inputs are finite; a program needn't handle non-finite values.
Results may differ from a plain program's by a relative error of at most 0.017.
Values may be sent and summed in bfloat16 or wider, within the bound.
A program may use at most 320 MiB of HBM per device.

v0:
```python
import functools
import math

import jax
import jax.numpy as jnp
import numpy as np
from jax import lax
from jax.experimental import pallas as pl
from jax.experimental.pallas import tpu as pltpu
from jax.sharding import PartitionSpec as P

HD = 64
BF = jnp.bfloat16
F32 = jnp.float32
MESH = pl.DeviceIdType.MESH


def norm_parts(values):
    center = values - jnp.mean(values, axis=-1, keepdims=True)
    spread = jnp.mean(center * center, axis=-1, keepdims=True)
    inv = lax.rsqrt(spread + 1e-05)
    return center * inv, inv


def norm_back(grad, xhat, inv, gain):
    q = grad * gain
    mean_q = jnp.mean(q, axis=-1, keepdims=True)
    mean_qx = jnp.mean(q * xhat, axis=-1, keepdims=True)
    return (q - mean_q - xhat * mean_qx) * inv, jnp.sum(grad * xhat, axis=0)


def mm(left, right):
    return jnp.dot(left, right, preferred_element_type=F32)


def mm_nt(left, right):
    return lax.dot_general(left, right, (((1,), (1,)), ((), ())), preferred_element_type=F32)


def mm_tn(left, right):
    return lax.dot_general(left, right, (((0,), (0,)), ((), ())), preferred_element_type=F32)


def softmax_rows(logits):
    shifted = logits - jnp.max(logits, axis=-1, keepdims=True)
    row_exp = jnp.exp(shifted)
    return row_exp / jnp.sum(row_exp, axis=-1, keepdims=True)


def gather_cuts(rows):
    return lax.all_gather(rows, "cuts", axis=0, tiled=True)


def scatter_cuts(rows):
    return lax.psum_scatter(rows.astype(BF), "cuts", scatter_dimension=0, tiled=True)


def columns_to_cuts(rows):
    return lax.all_to_all(rows, "cuts", split_axis=1, concat_axis=0, tiled=True)


def rows_to_cuts(rows):
    return lax.all_to_all(rows, "cuts", split_axis=0, concat_axis=1, tiled=True)


def ring_mod(index, count):
    return lax.rem(index, count)


def small_kernel(n_expert, n_cuts, src, out, by_expert, mine, by_cuts, send_a, recv_a, send_b, recv_b):
    me, cut = lax.axis_index("expert"), lax.axis_index("cuts")
    width = out.shape[1]
    barrier = pltpu.get_barrier_semaphore()
    for step in range(1, n_expert):
        peer = ring_mod(me + step, n_expert)
        pl.semaphore_signal(barrier, inc=1, device_id=(peer, cut), device_id_type=MESH)
    for step in range(1, n_cuts):
        peer = ring_mod(cut + step, n_cuts)
        pl.semaphore_signal(barrier, inc=1, device_id=(me, peer), device_id_type=MESH)
    pl.semaphore_wait(barrier, n_expert + n_cuts - 2)

    def part(owner):
        return src.at[:, pl.ds(pl.multiple_of(owner * width, 128), width)]

    copies = []
    for step in range(1, n_expert):
        peer = ring_mod(me + step, n_expert)
        copies.append(
            pltpu.make_async_remote_copy(
                src_ref=part(peer),
                dst_ref=by_expert.at[step],
                send_sem=send_a.at[step],
                recv_sem=recv_a.at[step],
                device_id=(peer, cut),
                device_id_type=MESH,
            )
        )
        copies[-1].start()
    total = src[:, pl.ds(pl.multiple_of(me * width, 128), width)]
    for step in range(1, n_expert):
        copies[step - 1].wait()
        total = total + by_expert[step]
    mine[...] = total
    copies = []
    for step in range(1, n_cuts):
        peer = ring_mod(cut + step, n_cuts)
        copies.append(
            pltpu.make_async_remote_copy(
                src_ref=mine,
                dst_ref=by_cuts.at[step],
                send_sem=send_b.at[step],
                recv_sem=recv_b.at[step],
                device_id=(me, peer),
                device_id_type=MESH,
            )
        )
        copies[-1].start()
    for step in range(1, n_cuts):
        copies[step - 1].wait()
        total = total + by_cuts[step]
    out[...] = total


def sum_small(values, n_expert, n_cuts):
    rows, features = values.shape
    width = features // n_expert
    pad = -width % 128
    if pad:
        values = jnp.pad(values.reshape(rows, n_expert, width), ((0, 0), (0, 0), (0, pad)))
        values = values.reshape(rows, n_expert * (width + pad))
    wide = width + pad
    summed = pl.pallas_call(
        functools.partial(small_kernel, n_expert, n_cuts),
        name="sum_small",
        out_shape=jax.ShapeDtypeStruct((rows, wide), F32),
        in_specs=[pl.BlockSpec(memory_space=pltpu.VMEM)],
        out_specs=pl.BlockSpec(memory_space=pltpu.VMEM),
        scratch_shapes=[
            pltpu.VMEM((n_expert, rows, wide), F32),
            pltpu.VMEM((rows, wide), F32),
            pltpu.VMEM((n_cuts, rows, wide), F32),
            pltpu.SemaphoreType.DMA((n_expert,)),
            pltpu.SemaphoreType.DMA((n_expert,)),
            pltpu.SemaphoreType.DMA((n_cuts,)),
            pltpu.SemaphoreType.DMA((n_cuts,)),
        ],
        compiler_params=pltpu.CompilerParams(collective_id=0, has_side_effects=True),
    )(values)
    return summed[:, :width]


def dot_nt(left, right):
    return lax.dot_general(left, right, (((1,), (1,)), ((), ())), preferred_element_type=F32)


def tile_of(step, size):
    return pl.ds(pl.multiple_of(step * size, size), size)


def lane_softmax(logits, low, high):
    lane = lax.broadcasted_iota(jnp.int32, logits.shape, 1)
    inside = (lane >= low) & (lane < high)
    kept = jnp.where(inside, logits, -1e30)
    powers = jnp.exp(kept - jnp.max(kept, axis=1, keepdims=True))
    powers = jnp.where(inside, powers, 0.0)
    return powers / jnp.sum(powers, axis=1, keepdims=True), lane


def mlp_both(rows, d_rows, w_up, w_down, act, d_up, write):
    root, cubic = math.sqrt(2.0 / math.pi), 0.044715

    @pl.loop(0, act.shape[1] // 256)
    def _(step):
        span = tile_of(step, 256)
        up = mm(rows[...], w_up[:, span])
        d_act = dot_nt(d_rows[...], w_down[span, :])
        square = up * up
        bent = jnp.tanh(root * up * (1.0 + cubic * square))
        half = 0.5 * (1.0 + bent)
        act[:, span] = (up * half).astype(BF)
        slope = half + 0.5 * up * (1.0 - bent * bent) * (root + 3.0 * root * cubic * square)
        d_up[:, span] = (d_act * slope).astype(BF)

    @pl.loop(0, w_up.shape[0] // 256)
    def _(step):
        span = tile_of(step, 256)
        write(span, mm(act[...], w_down[:, span]), dot_nt(d_up[...], w_up[span, :]))


def middle_kernel(
    sizes, slots, second, grad_all, grad_rows, w_in, w_out, small, sort, e_in, e_out,
    sums, ret_a, ret_b, o_in, o_out, rows_in, d_rows_all, act_e_all, d_first_all,
    sec, grd, win, wout, act, d_up, part_a, part_b, ffn_x, ffn_y, ffn_qa, ffn_qb,
    zbuf, rows, g_rows, d_rows, act_e, d_first, wi_e, wo_e, out_a, out_b, row_x, row_y, row_qa, row_qb, sorted_back, send_back,
    twin_in, level_in, fin_in,
    load_sem, weight_sem, store_sem, store_e_sem, z_sem, ag_sem, eag_sem, frs_sem, ers_sem, zr_sem,
    twin_sem, level_sem, fin_sem,
):
    n_expert, groups, here, slab = sizes
    me, cut = lax.axis_index("expert"), lax.axis_index("cuts")
    at_x, at_y, at_d = (jnp.bitwise_xor(cut, k) for k in (1, 2, 3))
    block = zbuf.shape[2]
    per_group = here // groups
    experts_all = n_expert * here

    def load(src, dst, index):
        copy = pltpu.make_async_copy(src, dst, load_sem.at[index])
        copy.start()
        return copy

    def remote(src, dst, sems, index, peer):
        return pltpu.make_async_remote_copy(
            src_ref=src, dst_ref=dst, send_sem=sems.at[0, index], recv_sem=sems.at[1, index],
            device_id=peer, device_id_type=MESH,
        )

    def send(src, dst, sems, index, peer):
        copy = remote(src, dst, sems, index, peer)
        copy.start()
        return copy

    loads = [
        load(second, sec.at[cut], 0), load(w_in, win, 1), load(w_out, wout, 2), load(grad_all, grd, 3),
    ]

    def fetch_expert(i):
        slot = i % 2
        copies = [
            pltpu.make_async_copy(e_in.at[i], wi_e.at[slot], weight_sem.at[0, slot]),
            pltpu.make_async_copy(e_out.at[i], wo_e.at[slot], weight_sem.at[1, slot]),
            pltpu.make_async_copy(grad_rows.at[i], g_rows.at[slot], weight_sem.at[2, slot]),
        ]
        for copy in copies:
            copy.start()
        return copies

    fetched = [fetch_expert(0), fetch_expert(1)]
    barrier = pltpu.get_barrier_semaphore()
    for k in range(1, n_expert):
        pl.semaphore_signal(barrier, inc=1, device_id=(jnp.bitwise_xor(me, k), cut), device_id_type=MESH)
    for peer in (at_x, at_y):
        pl.semaphore_signal(barrier, inc=1, device_id=(me, peer), device_id_type=MESH)
    pl.semaphore_signal(barrier, inc=1, device_id=(me, at_d), device_id_type=MESH)
    pl.semaphore_wait(barrier, n_expert + 2)
    core, level = lax.rem(me, 2), lax.div(me, 2)
    levels = n_expert // 2

    z_copies = []
    for g in range(groups):
        for k in range(1, n_expert):
            peer = jnp.bitwise_xor(me, k)
            z_copies.append(send(slots.at[g, peer], zbuf.at[g, me], z_sem, g * n_expert + k, (peer, cut)))
    loads[0].wait()
    ag = [
        send(sec.at[cut], sec.at[cut], ag_sem, 0, (me, at_x)),
        send(sec.at[cut], sec.at[cut], ag_sem, 1, (me, at_y)),
    ]
    half = sec.shape[1] // 2
    ag += [
        remote(sec.at[at_x, pl.ds(0, half)], sec.at[at_x, pl.ds(0, half)], ag_sem, 2, (me, at_y)),
        remote(sec.at[at_y, pl.ds(half, half)], sec.at[at_y, pl.ds(half, half)], ag_sem, 3, (me, at_x)),
    ]
    for g in range(groups):
        zbuf[g, me] = slots[g, me]
    def ffn_block(which, owner):
        mixing, lane = lane_softmax(mm(sec[owner], small[...]), experts_all, experts_all + 2)
        first_mix = jnp.sum(jnp.where(lane == experts_all, mixing, 0.0), axis=1, keepdims=True)
        grd[owner] = (grd[owner].astype(F32) * first_mix).astype(BF)

        def write(span, out, d_row):
            @pl.when(which == 0)
            def _():
                sums[0, :, span] = out
                sums[1, :, span] = d_row

            part_a[which, :, span] = out.astype(BF)
            part_b[which, :, span] = d_row.astype(BF)

        mlp_both(sec.at[owner], grd.at[owner], win, wout, act.at[owner], d_up.at[owner], write)

    def level_rows(index, half):
        return pl.ds(pl.multiple_of(index * 256 + half * 128, 128), 128)

    def weight_grad(m, left, right, held):
        @pl.loop(0, levels)
        def _(step):
            span = tile_of(step, 256)
            lhs = left[:, :, span].reshape(-1, 256)
            held[span, :] = mm_tn(lhs, right[...].reshape(-1, right.shape[2])).astype(BF)

        return [
            send(held.at[level_rows(n, 1 - core)], twin_in.at[m, n], twin_sem, m * levels + n, (jnp.bitwise_xor(me, 1), cut))
            for n in range(levels)
        ]

    def weight_sum(m, held, twins):
        for copy in twins:
            copy.wait_recv()

        @pl.loop(0, levels)
        def _(step):
            here_rows = level_rows(step, core)
            held[here_rows, :] = (held[here_rows, :].astype(F32) + twin_in[m, step].astype(F32)).astype(BF)

        copies = []
        for k in range(1, levels):
            peer = jnp.bitwise_xor(level, k)
            copies.append(
                send(
                    held.at[level_rows(peer, core)], level_in.at[m, k - 1], level_sem, m * (levels - 1) + k - 1,
                    (2 * peer + core, cut),
                )
            )
        return copies

    def weight_total(m, held, copies):
        for copy in copies:
            copy.wait_recv()
        total = held[level_rows(level, core), :].astype(F32)
        for k in range(1, levels):
            total = total + level_in[m, k - 1].astype(F32)
        return total.astype(BF)

    for copy in loads[1:]:
        copy.wait()
    def slab_of(owner):
        return pl.ds(pl.multiple_of(owner * slab, slab), slab)

    eag = {}
    cut_half = slab // 2
    for i in range(here):
        mine = rows.at[i, slab_of(cut)]
        from_x = rows.at[i, pl.ds(pl.multiple_of(at_x * slab, slab), cut_half)]
        from_y = rows.at[i, pl.ds(pl.multiple_of(at_y * slab + cut_half, cut_half), cut_half)]
        eag[i] = [
            remote(mine, mine, eag_sem, 4 * i, (me, at_x)),
            remote(mine, mine, eag_sem, 4 * i + 1, (me, at_y)),
            remote(from_x, from_x, eag_sem, 4 * i + 2, (me, at_y)),
            remote(from_y, from_y, eag_sem, 4 * i + 3, (me, at_x)),
        ]

    def relay(copies):
        copies[0].wait_recv()
        copies[2].start()
        copies[1].wait_recv()
        copies[3].start()

    @pl.loop(0, sec.shape[0])
    def _(which):
        @pl.when(which == 1)
        def _():
            relay(ag)

        @pl.when(which == 2)
        def _():
            for g in range(groups):
                for k in range(1, n_expert):
                    z_copies[g * (n_expert - 1) + k - 1].wait_recv()
                flat = zbuf[g].reshape(n_expert * block, zbuf.shape[3])
                for j in range(per_group):
                    i = g * per_group + j
                    rows[i, slab_of(cut)] = mm(sort[pl.ds(j * slab, slab), :], flat).astype(BF)
                    eag[i][0].start()
                    eag[i][1].start()

        @pl.when(which == 3)
        def _():
            ag[2].wait_recv()
            ag[3].wait_recv()
            relay(eag[0])

        ffn_block(which, jnp.bitwise_xor(cut, which))

    twins_in = weight_grad(0, sec, d_up, win)
    expert_stores = {}
    ers = {}

    def expert(i):
        slot = i % 2
        if i >= 2:
            for copy in expert_stores[i - 2]:
                copy.wait()
        for copy in fetched[i]:
            copy.wait()
        logits = mm(rows[i], small[...])
        router, lane = lane_softmax(logits, 0, experts_all)
        gate = jnp.sum(jnp.where(lane == me * here + i, router, 0.0), axis=1, keepdims=True)
        mixing, lane = lane_softmax(logits, experts_all, experts_all + 2)
        mixing = jnp.sum(jnp.where(lane == experts_all + 1, mixing, 0.0), axis=1, keepdims=True)
        d_rows[slot] = (g_rows[slot].astype(F32) * mixing * gate).astype(BF)

        def write(span, out, d_row):
            out_a[i, :, span] = out.astype(BF)
            out_b[i, :, span] = d_row.astype(BF)

        mlp_both(rows.at[i], d_rows.at[slot], wi_e.at[slot], wo_e.at[slot], act_e.at[slot], d_first.at[slot], write)
        expert_stores[i] = []
        for n, (src, dst) in enumerate(((d_rows, d_rows_all), (act_e, act_e_all), (d_first, d_first_all))):
            copy = pltpu.make_async_copy(src.at[slot], dst.at[i], store_e_sem.at[n, slot])
            copy.start()
            expert_stores[i].append(copy)
        ers[i] = [
            send(out_a.at[i, slab_of(at_x)], row_x.at[i, 0], ers_sem, 6 * i, (me, at_x)),
            send(out_a.at[i, slab_of(at_d)], row_x.at[i, 1], ers_sem, 6 * i + 1, (me, at_x)),
            send(out_b.at[i, slab_of(at_y)], row_y.at[i, 0], ers_sem, 6 * i + 2, (me, at_y)),
            send(out_b.at[i, slab_of(at_d)], row_y.at[i, 1], ers_sem, 6 * i + 3, (me, at_y)),
        ]

    def add_into(ref, *others):
        total = ref[...].astype(F32)
        for other in others:
            total = total + other[...].astype(F32)
        ref[...] = total.astype(BF)

    def pass_on(i):
        for copy in ers[i][:4]:
            copy.wait_recv()
        add_into(out_a.at[i, slab_of(at_y)], row_x.at[i, 1])
        add_into(out_b.at[i, slab_of(at_x)], row_y.at[i, 1])
        ers[i] += [
            send(out_a.at[i, slab_of(at_y)], row_qa.at[i], ers_sem, 6 * i + 4, (me, at_y)),
            send(out_b.at[i, slab_of(at_x)], row_qb.at[i], ers_sem, 6 * i + 5, (me, at_x)),
        ]

    back_copies = []

    def finish(i):
        ers[i][4].wait_recv()
        ers[i][5].wait_recv()
        for n, (out, near, far) in enumerate(((out_a, row_x, row_qa), (out_b, row_y, row_qb))):
            total = out[i, slab_of(cut)].astype(F32) + near[i, 0].astype(F32) + far[i].astype(F32)
            sorted_back[n, i] = total.astype(BF)
        if (i + 1) % per_group == 0:
            g = i // per_group
            for n in range(2):
                flat = sorted_back[n, pl.ds(g * per_group, per_group)].reshape(per_group * slab, -1)
                placed = mm_tn(sort[...], flat).astype(BF)
                send_back[n, g] = placed.reshape(n_expert, block, -1)
                (ret_a, ret_b)[n][g, me] = send_back[n, g, me]
                for k in range(1, n_expert):
                    peer = jnp.bitwise_xor(me, k)
                    back_copies.append(
                        send(
                            send_back.at[n, g, peer], (ret_a, ret_b)[n].at[g, me], zr_sem,
                            (n * groups + g) * n_expert + k, (peer, cut),
                        )
                    )

    for i in range(here):
        if i + 1 < here:
            relay(eag[i + 1])
        eag[i][2].wait_recv()
        eag[i][3].wait_recv()
        expert(i)
        if i + 2 < here:
            fetched.append(fetch_expert(i + 2))
        if i == 0:
            levels_in = weight_sum(0, win, twins_in)
            twins_out = weight_grad(1, act, grd, wout)
        if i == here - 1:
            frs = [
                send(part_a.at[1], ffn_x.at[0], frs_sem, 0, (me, at_x)),
                send(part_a.at[3], ffn_x.at[1], frs_sem, 1, (me, at_x)),
                send(part_b.at[2], ffn_y.at[0], frs_sem, 2, (me, at_y)),
                send(part_b.at[3], ffn_y.at[1], frs_sem, 3, (me, at_y)),
            ]
        if i == 1:
            levels_out = weight_sum(1, wout, twins_out)
        if i >= 1:
            pass_on(i - 1)
        if i >= 2:
            finish(i - 2)
    rows_store = pltpu.make_async_copy(rows, rows_in, store_sem.at[0])
    rows_store.start()
    pass_on(here - 1)
    finish(here - 2)
    finish(here - 1)
    for copy in frs[:4]:
        copy.wait_recv()
    add_into(part_a.at[2], ffn_x.at[1])
    add_into(part_b.at[1], ffn_y.at[1])
    frs += [
        send(part_a.at[2], ffn_qa, frs_sem, 4, (me, at_y)),
        send(part_b.at[1], ffn_qb, frs_sem, 5, (me, at_x)),
    ]
    fin_in[...] = weight_total(0, win, levels_in).reshape(fin_in.shape)
    fin_copies = []
    for k, peer in ((1, at_x), (2, at_y), (3, at_d)):
        fin_copies.append(send(fin_in.at[peer], o_in.at[cut], fin_sem, k - 1, (me, peer)))
    o_in[cut] = fin_in[cut]
    o_out[...] = weight_total(1, wout, levels_out)
    frs[4].wait_recv()
    frs[5].wait_recv()
    sums[0] = sums[0] + ffn_x[0].astype(F32) + ffn_qa[...].astype(F32)
    sums[1] = sums[1] + ffn_y[0].astype(F32) + ffn_qb[...].astype(F32)
    for copy in back_copies + fin_copies:
        copy.wait_recv()
    for copy in z_copies + ag + frs + back_copies + fin_copies + twins_in + twins_out + levels_in + levels_out:
        copy.wait_send()
    for i in range(here):
        for copy in eag[i] + ers[i]:
            copy.wait_send()
    for i in (here - 2, here - 1):
        for copy in expert_stores[i]:
            copy.wait()
    rows_store.wait()


def middle(slots, second, grad_all, grad_rows, w_in, w_out, small, sort, e_in, e_out, n_expert, n_cuts):
    groups, _, block, width = slots.shape
    tokens = second.shape[0]
    here, _, hidden = e_in.shape
    ffn = w_in.shape[1]
    slab = n_expert * block * groups // here
    rows = n_cuts * slab
    levels, deep = n_expert // 2, width // n_expert
    any_spec, vmem_spec = pl.BlockSpec(memory_space=pl.ANY), pl.BlockSpec(memory_space=pltpu.VMEM)
    shape = jax.ShapeDtypeStruct
    dma = pltpu.SemaphoreType.DMA
    flops = 8 * (n_cuts * tokens * ffn + here * rows * hidden) * width
    return pl.pallas_call(
        functools.partial(middle_kernel, (n_expert, groups, here, slab)),
        name="middle",
        out_shape=(
            shape((2, tokens, width), F32), shape((groups, n_expert, block, width), BF),
            shape((groups, n_expert, block, width), BF), shape((n_cuts, deep // n_cuts, ffn), BF), shape((deep, width), BF),
            shape((here, rows, width), BF), shape((here, rows, width), BF),
            shape((here, rows, hidden), BF), shape((here, rows, hidden), BF),
        ),
        in_specs=[vmem_spec] + [any_spec] * 5 + [vmem_spec] * 2 + [any_spec] * 2,
        out_specs=(vmem_spec,) * 5 + (any_spec,) * 4,
        scratch_shapes=[
            pltpu.VMEM((n_cuts, tokens, width), BF), pltpu.VMEM((n_cuts, tokens, width), BF),
            pltpu.VMEM((width, ffn), BF), pltpu.VMEM((ffn, width), BF),
            pltpu.VMEM((n_cuts, tokens, ffn), BF), pltpu.VMEM((n_cuts, tokens, ffn), BF),
            pltpu.VMEM((n_cuts, tokens, width), BF), pltpu.VMEM((n_cuts, tokens, width), BF),
            pltpu.VMEM((2, tokens, width), BF), pltpu.VMEM((2, tokens, width), BF),
            pltpu.VMEM((tokens, width), BF), pltpu.VMEM((tokens, width), BF),
            pltpu.VMEM((groups, n_expert, block, width), BF), pltpu.VMEM((here, rows, width), BF),
            pltpu.VMEM((2, rows, width), BF), pltpu.VMEM((2, rows, width), BF),
            pltpu.VMEM((2, rows, hidden), BF), pltpu.VMEM((2, rows, hidden), BF),
            pltpu.VMEM((2, width, hidden), BF), pltpu.VMEM((2, hidden, width), BF),
            pltpu.VMEM((here, rows, width), BF), pltpu.VMEM((here, rows, width), BF),
            pltpu.VMEM((here, 2, slab, width), BF), pltpu.VMEM((here, 2, slab, width), BF),
            pltpu.VMEM((here, slab, width), BF), pltpu.VMEM((here, slab, width), BF),
            pltpu.VMEM((2, here, slab, width), BF), pltpu.VMEM((2, groups, n_expert, block, width), BF),
            pltpu.VMEM((2, levels, deep, width), BF), pltpu.VMEM((2, levels - 1, deep, width), BF),
            pltpu.VMEM((n_cuts, deep // n_cuts, ffn), BF),
            dma((4,)), dma((3, 2)), dma((1,)), dma((3, 2)),
            dma((2, groups * n_expert)), dma((2, 4)), dma((2, 4 * here)), dma((2, 6)), dma((2, 6 * here)),
            dma((2, 2 * groups * n_expert)),
            dma((2, 2 * levels)), dma((2, 2 * (levels - 1))), dma((2, 3)),
        ],
        compiler_params=pltpu.CompilerParams(
            collective_id=1, has_side_effects=True, vmem_limit_bytes=67_000_000
        ),
        cost_estimate=pl.CostEstimate(flops=flops, bytes_accessed=48 << 20, transcendentals=0),
    )(slots, second, grad_all, grad_rows, w_in, w_out, small, sort, e_in, e_out)


def tail_kernel(
    heads, scaling, g_attn, d_heads, joined, lse, normed, qkv, source, gain, d_hidden, tiny,
    d_source, o_qkv, o_attn, o_tiny, o_gain,
    core_in, own, a_in, a_z, a_mine, gq, core_q, own_q, z_q, fin_q,
    dh, dj, acc_q, acc_k, acc_v, dn, dn_in, norm_v, qkv_v, tiny_e, tiny_m, tiny_c, late, late_e, late_m, late_c,
    load_sem, core_sem, z_sem, cut_sem, te_sem, tc_sem,
):
    me, cut = lax.axis_index("expert"), lax.axis_index("cuts")
    core, level = lax.rem(me, 2), lax.div(me, 2)
    other = 1 - core
    n_cuts, tokens, width = dh.shape
    n_expert = tiny_e.shape[0]
    levels = n_expert // 2
    twin = (jnp.bitwise_xor(me, 1), cut)

    def send(src, dst, sems, index, peer):
        copy = pltpu.make_async_remote_copy(
            src_ref=src, dst_ref=dst, send_sem=sems.at[0, index], recv_sem=sems.at[1, index],
            device_id=peer, device_id_type=MESH,
        )
        copy.start()
        return copy

    def load(src, dst, index):
        copy = pltpu.make_async_copy(src, dst, load_sem.at[index])
        copy.start()
        return copy

    mine = load(g_attn.at[:, core], own, 0)
    later = [load(normed, norm_v, 1), load(qkv, qkv_v, 2)]
    barrier = pltpu.get_barrier_semaphore()
    for k in range(1, n_expert):
        pl.semaphore_signal(barrier, inc=1, device_id=(jnp.bitwise_xor(me, k), cut), device_id_type=MESH)
    for k in range(1, n_cuts):
        pl.semaphore_signal(barrier, inc=1, device_id=(me, jnp.bitwise_xor(cut, k)), device_id_type=MESH)
    pl.semaphore_wait(barrier, n_expert + n_cuts - 2)

    def columns(index, size):
        return pl.ds(pl.multiple_of(index * size, size), size)

    sent = []

    def to_cuts(src_of, dst_of, base):
        copies = []
        for k in range(1, n_cuts):
            peer = jnp.bitwise_xor(cut, k)
            copies.append(send(src_of(peer), dst_of(k), cut_sem, base + k - 1, (me, peer)))
        sent.extend(copies)
        return copies

    def to_levels(src_of, dst_of, base):
        copies = []
        for k in range(1, levels):
            peer = jnp.bitwise_xor(level, k)
            copies.append(send(src_of(peer), dst_of(k), z_sem, base + k - 1, (2 * peer + core, cut)))
        sent.extend(copies)
        return copies

    def to_experts(src, dst, base):
        copies = []
        for k in range(1, n_expert):
            peer = jnp.bitwise_xor(me, k)
            copies.append(send(src.at[:, columns(peer, 128)], dst.at[k], te_sem, base + k - 1, (peer, cut)))
        sent.extend(copies)
        return copies

    heads_moved = to_cuts(lambda peer: d_heads.at[:, columns(peer, width)], lambda k: dh.at[cut], 0)
    twins = [send(g_attn.at[:, other], core_in, core_sem, 0, twin)]
    tiny_moved = to_experts(tiny, tiny_e, 0)
    dh[cut] = d_heads[:, columns(cut, width)]
    mine.wait()
    twins[0].wait_recv()

    @pl.loop(0, levels)
    def _(step):
        own[step] = (own[step].astype(F32) + core_in[step].astype(F32)).astype(BF)

    piece = own.shape[1] // n_cuts
    attn_moved = to_cuts(lambda peer: own.at[:, columns(peer, piece)], lambda k: a_in.at[k - 1], 3)

    acc_q[...] = jnp.zeros_like(acc_q)
    acc_k[...] = jnp.zeros_like(acc_k)
    acc_v[...] = jnp.zeros_like(acc_v)
    for copy in heads_moved:
        copy.wait_recv()

    @pl.loop(0, heads)
    def _(head):
        pair, half = lax.div(head, 2), lax.rem(head, 2)
        lane = lax.broadcasted_iota(jnp.int32, (1, 128), 1)
        keep = (lax.div(lane, HD) == half).astype(F32)
        keep_low = keep.astype(BF)
        cols = columns(pair, 128)
        k_cols = pl.ds(pl.multiple_of(width + pair * 128, 128), 128)
        v_cols = pl.ds(pl.multiple_of(2 * width + pair * 128, 128), 128)
        for i in range(n_cuts):
            reach = (i + 1) * tokens
            here = pl.ds(i * tokens, tokens)
            query = joined[here, cols] * keep_low
            d_out = dh[i, :, cols] * keep_low
            keys = joined[pl.ds(0, reach), k_cols]
            scores = mm_nt(keys, query) * scaling - lse[head, :, here]
            key_at = lax.broadcasted_iota(jnp.int32, scores.shape, 0)
            query_at = lax.broadcasted_iota(jnp.int32, scores.shape, 1) + i * tokens
            soft = jnp.exp(jnp.where(key_at <= query_at, scores, -1e30))
            d_soft = mm_nt(joined[pl.ds(0, reach), v_cols], d_out)
            delta = jnp.sum(soft * d_soft, axis=0, keepdims=True)
            d_scores = (soft * (d_soft - delta)).astype(BF)
            acc_v[pl.ds(0, reach), cols] += mm(soft.astype(BF), d_out)
            acc_k[pl.ds(0, reach), cols] += mm(d_scores, query)
            acc_q[here, cols] += mm_tn(d_scores, keys) * keep

    dj[:, pl.ds(0, width)] = (acc_q[...] * scaling).astype(BF)
    dj[:, pl.ds(width, width)] = (acc_k[...] * scaling).astype(BF)
    dj[:, pl.ds(2 * width, width)] = acc_v[...].astype(BF)
    for copy in later:
        copy.wait()
    dn_moved = []
    for k in (3, 1, 2):
        peer = jnp.bitwise_xor(cut, k)
        dn[k] = mm_nt(dj[columns(peer, tokens), :], qkv_v[...]).astype(BF)
        dn_moved.append(send(dn.at[k], dn_in.at[k - 1], cut_sem, 6 + k - 1, (me, peer)))
    sent.extend(dn_moved)

    @pl.loop(0, levels)
    def _(step):
        part = mm_tn(norm_v[:, columns(step, 256)], dj[...]).astype(BF)
        gq[step] = part.reshape(2, 128, part.shape[1])

    twins.append(send(gq.at[:, other], core_q, core_sem, 1, twin))
    d_normed = mm_nt(dj[columns(cut, tokens), :], qkv_v[...])

    for copy in attn_moved:
        copy.wait_recv()
    total = own[:, columns(cut, piece)].astype(F32)
    for k in range(1, n_cuts):
        total = total + a_in[k - 1].astype(F32)
    a_mine[...] = total.astype(BF)
    attn_z = to_levels(lambda peer: a_mine.at[peer], lambda k: a_z.at[k - 1], 0)

    twins[1].wait_recv()

    @pl.loop(0, levels)
    def _(step):
        own_q[step] = (gq[step, core].astype(F32) + core_q[step].astype(F32)).astype(BF)

    qkv_z = to_levels(lambda peer: own_q.at[peer], lambda k: z_q.at[k - 1], levels - 1)

    for copy in tiny_moved:
        copy.wait_recv()
    small = tiny[:, columns(me, 128)]
    for k in range(1, n_expert):
        small = small + tiny_e[k]
    tiny_m[...] = small

    def tiny_cuts(src, dst, base):
        copies = []
        for k in range(1, n_cuts):
            copies.append(send(src, dst.at[k], tc_sem, base + k - 1, (me, jnp.bitwise_xor(cut, k))))
        sent.extend(copies)
        return copies

    tiny_last = tiny_cuts(tiny_m, tiny_c, 0)

    for copy in dn_moved:
        copy.wait_recv()
    for k in range(1, n_cuts):
        d_normed = d_normed + dn_in[k - 1].astype(F32)
    xhat, inv = norm_parts(source[...].astype(F32))
    q = d_normed * gain[...]
    mean_q = jnp.mean(q, axis=-1, keepdims=True)
    mean_qx = jnp.mean(q * xhat, axis=-1, keepdims=True)
    d_source[...] = d_hidden[...] + (q - mean_q - xhat * mean_qx) * inv
    late[...] = jnp.broadcast_to(jnp.sum(d_normed * xhat, axis=0, keepdims=True), late.shape)
    late_moved = to_experts(late, late_e, n_expert - 1)

    for copy in tiny_last:
        copy.wait_recv()
    for k in range(1, n_cuts):
        small = small + tiny_c[k]
    o_tiny[...] = small

    for copy in late_moved:
        copy.wait_recv()
    small = late[:, columns(me, 128)]
    for k in range(1, n_expert):
        small = small + late_e[k]
    late_m[...] = small
    late_last = tiny_cuts(late_m, late_c, n_cuts - 1)

    for copy in attn_z:
        copy.wait_recv()
    total = a_mine[level].astype(F32)
    for k in range(1, levels):
        total = total + a_z[k - 1].astype(F32)
    o_attn[...] = total

    for copy in qkv_z:
        copy.wait_recv()
    total = own_q[level].astype(F32)
    for k in range(1, levels):
        total = total + z_q[k - 1].astype(F32)
    fin_q[...] = total.astype(BF).reshape(fin_q.shape)
    qkv_last = to_cuts(lambda peer: fin_q.at[peer], lambda k: o_qkv.at[cut], 9)
    o_qkv[cut] = fin_q[cut]

    for copy in late_last:
        copy.wait_recv()
    for k in range(1, n_cuts):
        small = small + late_c[k]
    o_gain[...] = small
    for copy in qkv_last:
        copy.wait_recv()
    for copy in sent + twins:
        copy.wait_send()


def tail(g_attn, d_heads, joined, lse, normed, qkv, source, gain, d_hidden, tiny, n_expert, n_cuts):
    tokens, features = d_heads.shape
    heads, seq_len = lse.shape
    levels, own = n_expert // 2, features // n_cuts
    deep = features // n_expert
    piece, wide = deep // n_cuts, 3 * own
    any_spec, vmem_spec = pl.BlockSpec(memory_space=pl.ANY), pl.BlockSpec(memory_space=pltpu.VMEM)
    shape, vmem, dma = jax.ShapeDtypeStruct, pltpu.VMEM, pltpu.SemaphoreType.DMA
    rows = tiny.shape[0]
    grid = (levels, 2, deep, features)
    return pl.pallas_call(
        functools.partial(tail_kernel, heads, HD ** (-0.5)),
        name="tail",
        out_shape=(
            shape((tokens, features), F32), shape((n_cuts, piece, wide), BF), shape((piece, features), F32), shape((rows, 128), F32), shape((8, 128), F32),
        ),
        in_specs=[any_spec] + [vmem_spec] * 3 + [any_spec] * 2 + [vmem_spec] * 4,
        out_specs=(vmem_spec,) * 5,
        scratch_shapes=[
            vmem((levels, deep, features), BF), vmem((levels, deep, features), BF),
            vmem((n_cuts - 1, levels, piece, features), BF),
            vmem((levels - 1, piece, features), BF), vmem((levels, piece, features), BF),
            vmem((levels, 2, deep, wide), BF), vmem((levels, deep, wide), BF), vmem((levels, deep, wide), BF),
            vmem((levels - 1, deep, wide), BF), vmem((n_cuts, piece, wide), BF),
            vmem((n_cuts, tokens, own), BF), vmem((seq_len, wide), BF),
            vmem((seq_len, own), F32), vmem((seq_len, own), F32), vmem((seq_len, own), F32),
            vmem((n_cuts, tokens, features), BF), vmem((n_cuts - 1, tokens, features), BF),
            vmem((seq_len, features), BF), vmem((features, wide), BF),
            vmem((n_expert, rows, 128), F32), vmem((rows, 128), F32), vmem((n_cuts, rows, 128), F32),
            vmem((8, features), F32), vmem((n_expert, 8, 128), F32), vmem((8, 128), F32), vmem((n_cuts, 8, 128), F32),
            dma((3,)), dma((2, 2)), dma((2, 2 * (levels - 1))), dma((2, 4 * (n_cuts - 1))),
            dma((2, 2 * (n_expert - 1))), dma((2, 2 * (n_cuts - 1))),
        ],
        compiler_params=pltpu.CompilerParams(
            collective_id=2, has_side_effects=True, vmem_limit_bytes=48 << 20
        ),
        cost_estimate=pl.CostEstimate(flops=20_000_000_000, bytes_accessed=24 << 20, transcendentals=0),
    )(
        g_attn.reshape(grid), d_heads, joined, lse.reshape(heads, 1, seq_len),
        normed, qkv, source, gain, d_hidden, tiny,
    )


def head_kernel(
    sizes, source, gains, small, info, sort, w_qkv, w_attn, w_in, cotangent,
    normed, qkv, joined, lse, head_out, attn_full, in_here, small_full, grad_all, grad_rows, placer, gains_all,
    src_v, qkv_v, norm_v, join_v, acc, heads_low, attn_v, in_v, cot_v, slots, zbuf, row_v,
    load_sem, store_sem, cut_sem, twin_sem, z_sem,
):
    heads, scaling, groups, here, slab = sizes
    me, cut = lax.axis_index("expert"), lax.axis_index("cuts")
    core = lax.rem(me, 2)
    twin = (jnp.bitwise_xor(me, 1), cut)
    at = [jnp.bitwise_xor(cut, k) for k in range(4)]
    n_cuts, tokens, width = src_v.shape
    n_expert, block = zbuf.shape[1], zbuf.shape[2]
    own, half, part = width // n_cuts, tokens // 2, tokens // 4

    def span(start, size, step):
        return pl.ds(pl.multiple_of(start, step), size)

    def remote(src, dst, sems, index, peer):
        return pltpu.make_async_remote_copy(
            src_ref=src, dst_ref=dst, send_sem=sems.at[0, index], recv_sem=sems.at[1, index],
            device_id=peer, device_id_type=MESH,
        )

    def local(src, dst, sems, index):
        copy = pltpu.make_async_copy(src, dst, sems.at[index])
        copy.start()
        return copy

    loads = [
        local(cotangent, cot_v, load_sem, 0),
        local(w_attn, attn_v, load_sem, 1),
        local(w_in.at[:, span(cut * width, width, width)], in_v, load_sem, 2),
    ]
    own_qkv = [
        local(
            w_qkv.at[:, span(n * width + cut * own, own, own)],
            qkv_v.at[span(cut * tokens, tokens, tokens), pl.ds(n * own, own)], load_sem, 3 + n,
        )
        for n in range(3)
    ]
    barrier = pltpu.get_barrier_semaphore()
    for k in range(1, n_expert):
        pl.semaphore_signal(barrier, inc=1, device_id=(jnp.bitwise_xor(me, k), cut), device_id_type=MESH)
    for k in range(1, n_cuts):
        pl.semaphore_signal(barrier, inc=1, device_id=(me, at[k]), device_id_type=MESH)
    pl.semaphore_wait(barrier, n_expert + n_cuts - 2)

    def gather(view, first, base):
        return [
            remote(first, view(cut), cut_sem, base, (me, at[1])),
            remote(first, view(cut), cut_sem, base + 1, (me, at[2])),
            remote(view(at[1], 0), view(at[1], 0), cut_sem, base + 2, (me, at[2])),
            remote(view(at[2], 1), view(at[2], 1), cut_sem, base + 3, (me, at[1])),
        ]

    def relay(copies):
        copies[0].wait_recv()
        copies[2].start()
        copies[1].wait_recv()
        copies[3].start()

    def whole(ref):
        def view(owner, piece=None):
            return ref.at[owner] if piece is None else ref.at[owner, pl.ds(piece * half, half)]

        return view

    def attn_view(owner, piece=None):
        start = owner * tokens + core * half
        if piece is None:
            return attn_full.at[span(start, half, half)]
        return attn_full.at[span(start + piece * part, part, part)]

    def slab_view(owner, piece=None):
        if piece is None:
            return grad_rows.at[:, span(owner * slab, slab, slab // 2)]
        return grad_rows.at[:, span(owner * slab + piece * (slab // 2), slab // 2, slab // 2)]

    def to_cuts(src_of, dst_of, base):
        return [remote(src_of(at[k]), dst_of(k), cut_sem, base + k - 1, (me, at[k])) for k in (3, 1, 2)]

    tokens_moved = gather(whole(src_v), source, 0)
    gains_moved = to_cuts(lambda peer: gains, lambda k: gains_all.at[cut], 16)
    small_moved = to_cuts(lambda peer: small, lambda k: small_full.at[cut], 19)
    qkv_moved = []
    for n in range(3):
        qkv_moved += to_cuts(
            lambda peer: w_qkv.at[span(core * half, half, half), span(n * width + peer * own, own, own)],
            lambda k: qkv_v.at[span(cut * tokens + core * half, half, half), pl.ds(n * own, own)],
            22 + 3 * n,
        )
    for copy in gains_moved + tokens_moved[:2] + qkv_moved + small_moved:
        copy.start()
    grad_moved = gather(whole(grad_all), cot_v, 4)
    attn_moved = gather(attn_view, attn_v.at[span(core * half, half, half)], 8)
    slab_moved = gather(slab_view, row_v, 12)
    in_moved = to_cuts(
        lambda peer: w_in.at[span(core * half, half, half), span(peer * width, width, width)],
        lambda k: in_here.at[span(cut * tokens + core * half, half, half)], 31,
    )
    head_moved = to_cuts(
        lambda peer: heads_low.at[span(peer * tokens, tokens, tokens)],
        lambda k: head_out.at[:, span(cut * own, own, own)], 34,
    )

    loads[0].wait()
    lane = lax.broadcasted_iota(jnp.int32, (tokens, 128), 1).astype(F32)
    picked = jnp.where(lane == info[:, 0:1], info[:, 1:2], 0.0)
    down = lax.broadcasted_iota(jnp.int32, (tokens, tokens), 0)
    right = lax.broadcasted_iota(jnp.int32, (tokens, tokens), 1)
    running = mm((down >= right).astype(F32).astype(BF), picked.astype(BF))
    target = info[:, 2:3] + jnp.sum(picked * running, axis=1, keepdims=True) - 1.0
    column = lax.broadcasted_iota(jnp.int32, placer.shape, 1).astype(F32)
    placer[...] = jnp.where(column == target, info[:, 1:2], 0.0).astype(BF)
    slots[...] = mm_tn(placer[...], cot_v[...]).astype(BF).reshape(slots.shape)
    z_moved = []
    for g in range(groups):
        for k in range(1, n_expert):
            peer = jnp.bitwise_xor(me, k)
            z_moved.append(remote(slots.at[g, peer], zbuf.at[g, me], z_sem, g * n_expert + k, (peer, cut)))
            z_moved[-1].start()
        zbuf[g, me] = slots[g, me]
    src_v[cut] = source[...]
    gains_all[cut] = gains[...]
    small_full[cut] = small[...]
    relay(tokens_moved)
    for copy in loads[1:] + own_qkv:
        copy.wait()
    stores = [
        local(cot_v, grad_all.at[cut], store_sem, 0),
        local(attn_v, attn_full.at[span(cut * tokens, tokens, tokens)], store_sem, 1),
        local(in_v, in_here.at[span(cut * tokens, tokens, tokens)], store_sem, 2),
    ]
    for copy in gains_moved:
        copy.wait_recv()

    def normalize(index):
        xhat, _ = norm_parts(src_v[index].astype(F32))
        for n in range(n_cuts):
            cols = slice(n * own, (n + 1) * own)
            norm_v[index, :, cols] = (xhat[:, cols] * gains_all[n, 0:1, :]).astype(BF)

    normalize(cut)
    normalize(at[1])
    normalize(at[2])
    for copy in qkv_moved:
        copy.wait_recv()

    def share(ref, base):
        copies = []
        for k in range(1, n_cuts):
            view = ref.at[span(at[k] * tokens + core * half, half, half)]
            copies.append(remote(view, view, twin_sem, base + k - 1, twin))
            copies[-1].start()
        return copies

    shared = share(qkv_v, 0)
    for copy in tokens_moved[2:]:
        copy.wait_recv()
    for copy in grad_moved[:2] + attn_moved[:2] + in_moved:
        copy.start()
    normalize(at[3])
    for copy in shared:
        copy.wait_recv()

    @pl.loop(0, n_cuts)
    def _(step):
        join_v[step] = mm(norm_v[step], qkv_v[...]).astype(BF)

    stores += [
        local(norm_v, normed, store_sem, 3), local(qkv_v, qkv, store_sem, 4), local(join_v, joined, store_sem, 5),
    ]
    acc[...] = jnp.zeros_like(acc)
    per_group = here // groups
    for copy in z_moved:
        copy.wait_recv()
    for g in range(groups):
        flat = zbuf[g].reshape(n_expert * block, width)
        for j in range(per_group):
            row_v[g * per_group + j] = mm(sort[pl.ds(j * slab, slab), :], flat).astype(BF)
    stores.append(local(row_v, slab_view(cut), store_sem, 6))

    @pl.loop(0, heads)
    def _(head):
        @pl.when(head == 2)
        def _():
            relay(grad_moved)
            relay(attn_moved)
            for copy in slab_moved[:2]:
                copy.start()

        pair = lax.div(head, 2)
        lane = lax.broadcasted_iota(jnp.int32, (1, 128), 1)
        keep = (lax.div(lane, HD) == lax.rem(head, 2)).astype(F32)
        keep_low = keep.astype(BF)
        cols = span(pair * 128, 128, 128)
        k_cols = span(own + pair * 128, 128, 128)
        v_cols = span(2 * own + pair * 128, 128, 128)
        for i in range(n_cuts):
            reach = (i + 1) * tokens
            query = join_v[i, :, cols] * keep_low
            keys = join_v[pl.ds(0, i + 1), :, k_cols].reshape(reach, 128)
            values = join_v[pl.ds(0, i + 1), :, v_cols].reshape(reach, 128)
            scores = mm_nt(keys, query) * scaling
            key_at = lax.broadcasted_iota(jnp.int32, scores.shape, 0)
            query_at = lax.broadcasted_iota(jnp.int32, scores.shape, 1) + i * tokens
            scores = jnp.where(key_at <= query_at, scores, -1e30)
            peak = jnp.max(scores, axis=0, keepdims=True)
            powers = jnp.exp(scores - peak)
            total = jnp.sum(powers, axis=0, keepdims=True)
            lse[head, :, pl.ds(i * tokens, tokens)] = peak + jnp.log(total)
            soft = (powers / total).astype(BF)
            acc[pl.ds(i * tokens, tokens), cols] += mm_tn(soft, values) * keep

    heads_low[...] = acc[...].astype(BF)
    for copy in head_moved:
        copy.start()
    head_out[:, span(cut * own, own, own)] = heads_low[span(cut * tokens, tokens, tokens), :]
    for copy in in_moved:
        copy.wait_recv()
    shared += share(in_here, 3)
    for copy in attn_moved[2:]:
        copy.wait_recv()
    shared += share(attn_full, 6)
    relay(slab_moved)
    for copy in shared[3:] + grad_moved[2:] + slab_moved[2:] + head_moved + small_moved:
        copy.wait_recv()
    for copy in stores:
        copy.wait()
    everything = tokens_moved + gains_moved + small_moved + qkv_moved + grad_moved + attn_moved + slab_moved
    for copy in everything + in_moved + head_moved + z_moved + shared:
        copy.wait_send()


def head(source, gains, small, info, sort, w_qkv, w_attn, w_in, cotangent, here, groups, capacity, n_expert, n_cuts):
    tokens, features = source.shape
    seq_len, own = tokens * n_cuts, features // n_cuts
    heads, slab = own // HD, n_expert * capacity
    block = here // groups * capacity
    any_spec, vmem_spec = pl.BlockSpec(memory_space=pl.ANY), pl.BlockSpec(memory_space=pltpu.VMEM)
    shape, vmem, dma = jax.ShapeDtypeStruct, pltpu.VMEM, pltpu.SemaphoreType.DMA
    slots = n_expert * groups * block
    return pl.pallas_call(
        functools.partial(head_kernel, (heads, HD ** (-0.5), groups, here, slab)),
        name="head",
        out_shape=(
            shape((n_cuts, tokens, features), BF), shape((features, 3 * own), BF), shape((n_cuts, tokens, 3 * own), BF),
            shape((heads, 1, seq_len), F32), shape((tokens, features), BF), shape((features, features), BF),
            shape((features, w_in.shape[1] // n_cuts), BF), shape((n_cuts,) + small.shape, BF),
            shape((n_cuts, tokens, features), BF), shape((here, n_cuts * slab, features), BF),
            shape((tokens, slots), BF), shape((n_cuts,) + gains.shape, F32),
        ),
        in_specs=[vmem_spec] * 5 + [any_spec] * 4,
        out_specs=(any_spec,) * 3 + (vmem_spec,) * 2 + (any_spec,) * 2 + (vmem_spec,) + (any_spec,) * 2 + (vmem_spec,) * 2,
        scratch_shapes=[
            vmem((n_cuts, tokens, features), BF), vmem((features, 3 * own), BF), vmem((n_cuts, tokens, features), BF),
            vmem((n_cuts, tokens, 3 * own), BF), vmem((seq_len, own), F32), vmem((seq_len, own), BF),
            vmem((tokens, features), BF), vmem((tokens, features), BF), vmem((tokens, features), BF),
            vmem((groups, n_expert, block, features), BF), vmem((groups, n_expert, block, features), BF),
            vmem((here, slab, features), BF),
            dma((6,)), dma((7,)), dma((2, 37)), dma((2, 9)), dma((2, groups * n_expert)),
        ],
        compiler_params=pltpu.CompilerParams(
            collective_id=3, has_side_effects=True, vmem_limit_bytes=48 << 20
        ),
        cost_estimate=pl.CostEstimate(flops=8_000_000_000, bytes_accessed=24 << 20, transcendentals=0),
    )(source, gains, small, info, sort, w_qkv, w_attn, w_in, cotangent)


def expert_grads_kernel(rows, d_first, act, d_rows, grad_in, grad_out):
    grad_in[0] = mm_tn(rows[0], d_first[0])
    grad_out[0] = mm_tn(act[0], d_rows[0])


def expert_grads(rows, d_first, act, d_rows):
    here, count, width = rows.shape
    hidden = act.shape[2]
    part = pl.BlockSpec((1, count, 256), lambda e, t: (e, 0, t))
    return pl.pallas_call(
        expert_grads_kernel,
        name="expert_grads",
        grid=(here, width // 256),
        out_shape=(jax.ShapeDtypeStruct((here, width, hidden), F32), jax.ShapeDtypeStruct((here, hidden, width), F32)),
        in_specs=[
            part, pl.BlockSpec((1, count, hidden), lambda e, t: (e, 0, 0)),
            part, pl.BlockSpec((1, count, width), lambda e, t: (e, 0, 0)),
        ],
        out_specs=(
            pl.BlockSpec((1, 256, hidden), lambda e, t: (e, t, 0)), pl.BlockSpec((1, 256, width), lambda e, t: (e, t, 0)),
        ),
        compiler_params=pltpu.CompilerParams(vmem_limit_bytes=32 << 20),
        cost_estimate=pl.CostEstimate(flops=4 * here * count * width * hidden, bytes_accessed=46 << 20, transcendentals=0),
    )(rows, d_first, act, d_rows)


def shards(
    block_input,
    routes,
    kept_mask,
    w_qkv,
    w_attn_out,
    w_in,
    w_out,
    w_router,
    w_mix,
    gain_attn,
    gain_ffn,
    expert_in,
    expert_out,
    cotangent,
):
    tokens, features = block_input.shape
    n_cuts = lax.axis_size("cuts")
    n_expert = lax.axis_size("expert")
    seq_len = tokens * n_cuts
    scaling = HD ** (-0.5)
    own = features // n_cuts
    heads = own // HD
    experts_all = w_router.shape[1]
    experts_here = expert_in.shape[0]
    capacity = 3 * tokens // (2 * experts_all)

    onehot = (routes[:, None] == jnp.arange(experts_all, dtype=jnp.int32)[None, :]).astype(F32)
    fused = n_cuts == 4
    groups = 2 if fused else 1
    per_group = experts_here // groups
    block = per_group * capacity
    owner, local = routes // experts_here, routes % experts_here
    start = (local // per_group) * (n_expert * block) + owner * block + local % per_group * capacity
    if not fused:
        onehot_kept = onehot * kept_mask.astype(F32)[:, None]
        lower_tri = (jnp.arange(tokens)[:, None] >= jnp.arange(tokens)[None, :]).astype(BF)
        running = mm(lower_tri, onehot_kept.astype(BF))
        slot_num = jnp.sum(onehot_kept * running, axis=1) - 1.0
        target = start.astype(F32) + slot_num
        columns = jnp.arange(experts_all * capacity, dtype=jnp.int32).astype(F32)
        placer = ((columns[None, :] == target[:, None]) & (kept_mask[:, None] > 0)).astype(BF)

    def to_owners(rows):
        grid = mm_tn(placer, rows).astype(BF).reshape(groups, n_expert, block, features)
        grid = grid.swapaxes(0, 1).reshape(n_expert, experts_here, capacity, features)
        moved = lax.all_to_all(grid, "expert", split_axis=0, concat_axis=2, tiled=True)
        return lax.all_gather(moved, "cuts", axis=2, tiled=True)[0]

    def to_sources(rows):
        summed = lax.psum_scatter(rows[None].astype(BF), "cuts", scatter_dimension=2, tiled=True)
        moved = lax.all_to_all(summed, "expert", split_axis=2, concat_axis=0, tiled=True)
        return mm(placer, moved.reshape(-1, features))

    inputs = block_input.astype(F32)
    if fused:
        pair = jnp.stack([gain_attn, gain_ffn], axis=0).astype(F32)
        small_here = jnp.concatenate([w_router, w_mix], axis=1)
        small_cols = small_here.shape[1]
        at = np.arange(n_expert * block)
        slab = n_expert * capacity
        goal = at % slab // capacity * block + at // slab * capacity + at % capacity
        sort = np.asarray(goal[:, None] == at[None, :], dtype=BF)
        info = jnp.stack([routes, kept_mask, start], axis=1).astype(F32)
        normed, qkv_here, joined, log_norm, head_out, attn_full, in_here, small_wide, grad_all, grad_rows, placer, gains = head(
            block_input, jnp.pad(pair, ((0, 6), (0, 0))), jnp.pad(small_here, ((0, 0), (0, -small_cols % 128))),
            info, jnp.asarray(sort), w_qkv, w_attn_out, w_in, cotangent,
            experts_here, groups, capacity, n_expert, n_cuts,
        )
        normed, joined = normed.reshape(seq_len, features), joined.reshape(seq_len, 3 * own)
        small_wide = small_wide.reshape(features, -1)
        small_full = small_wide[:, :small_cols]
        gain_one, gain_two = gains[:, 0].reshape(features), gains[:, 1].reshape(features)
    else:
        gains = gather_cuts(jnp.stack([gain_attn, gain_ffn], axis=1)).astype(F32)
        gain_one, gain_two = gains[:, 0], gains[:, 1]
        xhat_one, inv_one = norm_parts(inputs)
        normed = gather_cuts((xhat_one * gain_one).astype(BF))
        qkv_here = lax.all_to_all(
            w_qkv.reshape(own, 3, n_cuts, own), "cuts", split_axis=2, concat_axis=0, tiled=True
        ).reshape(features, 3 * own)
        joined = mm(normed, qkv_here).astype(BF)
        split = joined.reshape(seq_len, 3, heads, HD)
        q_heads, k_heads, v_heads = split[:, 0], split[:, 1], split[:, 2]
        spots = jnp.arange(seq_len, dtype=jnp.int32)
        visible = (spots[None, :] <= spots[:, None])[None]

        def masked_scores():
            scores = jnp.einsum("qhd,khd->hqk", q_heads, k_heads, preferred_element_type=F32) * scaling
            return jnp.where(visible, scores, -1e30)

        scores = masked_scores()
        peak = jnp.max(scores, axis=-1, keepdims=True)
        row_exp = jnp.exp(scores - peak)
        total = jnp.sum(row_exp, axis=-1, keepdims=True)
        weights_p = (row_exp / total).astype(BF)
        heads_here = jnp.einsum("hqk,khd->qhd", weights_p, v_heads, preferred_element_type=F32)
        log_norm = peak + jnp.log(total)
        head_out = rows_to_cuts(heads_here.reshape(seq_len, own).astype(BF))
        attn_full = gather_cuts(w_attn_out)
        small_full = gather_cuts(jnp.concatenate([w_router, w_mix], axis=1))
        grad_all = gather_cuts(cotangent)
        grad_rows = to_owners(cotangent)
        in_here = columns_to_cuts(w_in)
    hidden = inputs + mm(head_out, attn_full)
    xhat_two, inv_two = norm_parts(hidden)
    second = (xhat_two * gain_two).astype(BF)

    logits = mm(second, small_full)
    router_p = softmax_rows(logits[:, :experts_all])
    mixing = softmax_rows(logits[:, experts_all:])
    gate = jnp.sum(router_p * onehot, axis=1)
    grad = cotangent.astype(F32)
    d_moe = grad * mixing[:, 1:2]

    if fused:
        slots = mm_tn(placer, second).astype(BF).reshape(groups, n_expert, block, features)
        sums, ret_a, ret_b, s_in, s_out, rows_in, d_rows, expert_low, d_first = middle(
            slots, second, grad_all, grad_rows, in_here, w_out, small_wide, jnp.asarray(sort),
            expert_in, expert_out, n_expert, n_cuts,
        )
        dense, d_second_ffn = sums[0], sums[1]
        g_expert_in, g_expert_out = expert_grads(rows_in, d_first, expert_low, d_rows)
        picked = mm(placer, ret_a.reshape(-1, features))
        d_picked_in = mm(placer, ret_b.reshape(-1, features))
    else:
        rows_in = to_owners(second)
        row_logits = jnp.einsum("erd,dk->erk", rows_in, small_full, preferred_element_type=F32)
        ids = lax.axis_index("expert") * experts_here + jnp.arange(experts_here, dtype=jnp.int32)
        is_here = (jnp.arange(experts_all, dtype=jnp.int32)[None, :] == ids[:, None]).astype(F32)
        row_gate = jnp.sum(
            softmax_rows(row_logits[:, :, :experts_all]) * is_here[:, None, :], axis=2, keepdims=True
        )
        row_mixing = softmax_rows(row_logits[:, :, experts_all:])[:, :, 1:2]
        d_rows = (grad_rows.astype(F32) * row_mixing * row_gate).astype(BF)

        first = jnp.einsum("erd,edh->erh", rows_in, expert_in, preferred_element_type=F32)
        expert_act, expert_pull = jax.vjp(jax.nn.gelu, first)
        expert_low = expert_act.astype(BF)
        partial_out = jnp.einsum("erh,ehd->erd", expert_low, expert_out, preferred_element_type=F32)
        picked = to_sources(partial_out)

        second_all = gather_cuts(second)
        mixing_all = softmax_rows(mm(second_all, small_full[:, experts_all:]))
        d_dense_all = (grad_all.astype(F32) * mixing_all[:, 0:1]).astype(BF)
        up_proj = mm(second_all, in_here)
        activ, gelu_pull = jax.vjp(jax.nn.gelu, up_proj)
        activ_low = activ.astype(BF)
        dense = scatter_cuts(mm(activ_low, w_out)).astype(F32)
        d_activ = mm_nt(d_dense_all, w_out)
        g_out = mm_tn(activ_low, d_dense_all)
        d_up = gelu_pull(d_activ)[0].astype(BF)
        g_in = mm_tn(second_all, d_up)
        d_second_ffn = scatter_cuts(mm_nt(d_up, in_here)).astype(F32)

        d_expert_act = jnp.einsum("erd,ehd->erh", d_rows, expert_out, preferred_element_type=F32)
        d_first = expert_pull(d_expert_act)[0].astype(BF)
        d_rows_in = jnp.einsum("erh,edh->erd", d_first, expert_in, preferred_element_type=F32)
        g_expert_out = jnp.einsum("erh,erd->ehd", expert_low, d_rows, preferred_element_type=F32)
        g_expert_in = jnp.einsum("erd,erh->edh", rows_in, d_first, preferred_element_type=F32)
        d_picked_in = to_sources(d_rows_in)

    moe_val = gate[:, None] * picked
    block_out = (hidden + mixing[:, 0:1] * dense + mixing[:, 1:2] * moe_val).astype(BF)
    d_mixing = jnp.stack([jnp.sum(grad * dense, axis=1), jnp.sum(grad * moe_val, axis=1)], axis=1)
    d_gate = jnp.sum(d_moe * picked, axis=1)
    d_router = router_p * (onehot - gate[:, None]) * d_gate[:, None]
    d_mix = mixing * (d_mixing - jnp.sum(mixing * d_mixing, axis=1, keepdims=True))
    d_small = jnp.concatenate([d_router, d_mix], axis=1).astype(BF)
    g_small = mm_tn(d_small, second)
    d_second = d_second_ffn + mm_nt(d_small, small_full) + d_picked_in
    d_hidden_norm, g_gain_two = norm_back(d_second, xhat_two, inv_two, gain_two)
    d_hidden = grad + d_hidden_norm
    d_attn = d_hidden.astype(BF)
    g_attn_out = mm_tn(head_out, d_attn)
    d_head_rows = mm_nt(d_attn, attn_full).astype(BF)
    if fused:
        tiny = jnp.concatenate([g_small, g_gain_two[None, :]], axis=0)
        tiny = jnp.pad(tiny, ((0, -tiny.shape[0] % 8), (0, 0)))
        d_block_input, s_qkv, s_attn_out, tiny, late = tail(
            g_attn_out.astype(BF), d_head_rows, joined, log_norm[:, 0], normed,
            qkv_here, block_input, gain_one[None, :], d_hidden, tiny, n_expert, n_cuts,
        )
        swap = [
            ((flat % n_expert) * n_cuts + flat // n_expert, flat) for flat in range(n_expert * n_cuts)
        ]
        s_out = lax.ppermute(s_out, ("expert", "cuts"), swap).astype(F32)
        s_in = s_in.swapaxes(0, 1).reshape(-1, w_in.shape[1]).astype(F32)
        s_qkv = s_qkv.reshape(n_cuts, -1, 3, own).transpose(1, 2, 0, 3).reshape(-1, 3 * features).astype(F32)
        width = features // (n_expert * n_cuts)
        spot = lax.axis_index("cuts") * width
        s_tiny = lax.dynamic_slice_in_dim(tiny, spot, width, axis=1)
        s_late = lax.dynamic_slice_in_dim(late, spot, width, axis=1)
        return (
            block_out,
            d_block_input,
            s_qkv,
            s_attn_out,
            s_in,
            s_out,
            s_tiny[:experts_all].T,
            s_tiny[experts_all : experts_all + 2].T,
            s_late[0],
            s_tiny[experts_all + 2],
            g_expert_in,
            g_expert_out,
        )
    d_heads = columns_to_cuts(d_head_rows).reshape(seq_len, heads, HD)

    soft_p = jnp.exp(masked_scores() - log_norm)
    d_soft = jnp.einsum("qhd,khd->hqk", d_heads, v_heads, preferred_element_type=F32)
    delta = jnp.sum(soft_p * d_soft, axis=-1, keepdims=True)
    d_scores = (soft_p * (d_soft - delta)).astype(BF)
    d_query = jnp.einsum("hqk,khd->qhd", d_scores, k_heads, preferred_element_type=F32) * scaling
    d_keys = jnp.einsum("hqk,qhd->khd", d_scores, q_heads, preferred_element_type=F32) * scaling
    d_values = jnp.einsum("hqk,qhd->khd", soft_p.astype(BF), d_heads, preferred_element_type=F32)
    d_joined = jnp.stack([d_query, d_keys, d_values], axis=1).reshape(seq_len, 3 * own).astype(BF)
    g_qkv = mm_tn(normed, d_joined)
    d_normed = scatter_cuts(mm_nt(d_joined, qkv_here)).astype(F32)
    d_input_norm, g_gain_one = norm_back(d_normed, xhat_one, inv_one, gain_one)
    d_block_input = d_hidden + d_input_norm

    def over_experts(part):
        return lax.psum_scatter(part.astype(BF), "expert", scatter_dimension=0, tiled=True)

    s_in = rows_to_cuts(over_experts(g_in)).astype(F32)
    s_out = over_experts(g_out)
    swap = [
        ((flat % n_expert) * n_cuts + flat // n_expert, flat) for flat in range(n_expert * n_cuts)
    ]
    s_out = lax.ppermute(s_out, ("expert", "cuts"), swap).astype(F32)
    s_qkv = over_experts(g_qkv)
    deep = s_qkv.shape[0]
    s_qkv = lax.all_to_all(
        s_qkv.reshape(deep, 3, 1, own), "cuts", split_axis=0, concat_axis=2, tiled=True
    )
    s_qkv = s_qkv.reshape(-1, 3 * features).astype(F32)
    s_attn_out = scatter_cuts(over_experts(g_attn_out)).astype(F32)
    tiny = jnp.concatenate([g_small, g_gain_one[None, :], g_gain_two[None, :]], axis=0)
    tiny = jnp.pad(tiny, ((0, -tiny.shape[0] % 8), (0, 0)))
    tiny = sum_small(tiny, n_expert, n_cuts)
    width = features // (n_expert * n_cuts)
    s_tiny = lax.dynamic_slice_in_dim(tiny, lax.axis_index("cuts") * width, width, axis=1)
    return (
        block_out,
        d_block_input,
        s_qkv,
        s_attn_out,
        s_in,
        s_out,
        s_tiny[:experts_all].T,
        s_tiny[experts_all : experts_all + 2].T,
        s_tiny[experts_all + 2],
        s_tiny[experts_all + 3],
        g_expert_in,
        g_expert_out,
    )


def solution(mesh):
    both = ("expert", "cuts")
    placed = (
        P(both, None),
        P(both),
        P(both),
        P("cuts", None),
        P("cuts", None),
        P("cuts", None),
        P("cuts", None),
        P("cuts", None),
        P("cuts", None),
        P("cuts"),
        P("cuts"),
        P("expert", None, "cuts"),
        P("expert", "cuts", None),
        P(both, None),
    )
    results = (
        P(both, None),
        P(both, None),
        P(both, None),
        P(both, None),
        P(both, None),
        P(both, None),
        P(both, None),
        P(both, None),
        P(both),
        P(both),
        P("expert", None, "cuts"),
        P("expert", "cuts", None),
    )
    return jax.shard_map(
        shards, mesh=mesh, in_specs=placed, out_specs=results, check_vma=False
    )
```

profile of v0, /device:TPU:0, one launch (start us, length us, event | category | flops | bytes accessed | tf_op | source)
XLA Modules:
  0.0 369.0 jit_solution(5716618572062968168)
XLA Ops:
  2.7 0.7 pad_maximum_fusion
  4.4 1.0 copy-done.6
  5.5 1.0 copy-done.8
  6.5 1.0 copy-done.10
  7.6 0.9 copy-done.13
  8.4 107.0 %head.1 = (bf16[4,256,1024]{2,1,0:T(8,128)(2,1)}, bf16[1024,768]{1,0:T(8,128)(2,1)S(1)}, bf16[4,256,768]{2,1,0:T(8,128)(2,1)S(1)}, f32[4,1,1024]{2,1,0:T(1,128)S...) custom-call(bf16[256,1024]{1,0:T(8,128)(2,1)S(1)} %copy-done.8, ...), custom_call_target="tpu_custom_call" | custom-call | flops 8000000000 | bytes 25165824 | tf_op jit(solution)/shard_map/head/pallas_call | solution.py:1064
  115.5 3.8 %fusion.26 = (f32[256]{0:T(256)S(1)}, f32[256,1024]{1,0:T(8,128)S(1)}) fusion(bf16[256,1024]{1,0:T(8,128)(2,1)S(1)} %get-tuple-element.40, bf16[1024,1024]{1,0:T(8,128)(2,1)} %get-tuple-element.41, bf16[256,1024]{1,0:T(8,128)(2,1)S(1)} %copy-done.8), kind=kOutput, calls=%fused_computation.80 | convolution fusion | flops 537657088 | bytes 4195328 | tf_op jit(solution)/shard_map/dot_general | solution.py:33
  119.9 1.3 convolution_convert_fusion.1
  121.2 147.3 %middle.1 = (f32[2,256,1024]{2,1,0:T(8,128)}, bf16[2,8,24,1024]{3,2,1,0:T(8,128)(2,1)}, bf16[2,8,24,1024]{3,2,1,0:T(8,128)(2,1)}, bf16[4,32,1024]{2,1,0:T(8,128)...) custom-call(bf16[2,8,24,1024]{3,2,1,0:T(8,128)(2,1)} %bitcast.61, ...), custom_call_target="tpu_custom_call" | custom-call | flops 21474836480 | bytes 50331648 | tf_op jit(solution)/shard_map/middle/pallas_call | solution.py:521
  268.5 3.6 collective-permute-start
  272.0 1.4 fusion.10
  273.6 3.6 fusion.1
  280.0 1.1 copy-done.21
  281.1 0.8 convolution_convert_fusion.2.d_heads
  282.2 2.1 convolution_convert_fusion
  284.3 0.8 convert_bitcast_fusion
  285.2 1.4 copy-done.12
  286.6 57.0 %tail.1 = (f32[256,1024]{1,0:T(8,128)S(1)}, bf16[4,32,768]{2,1,0:T(8,128)(2,1)S(1)}, f32[32,1024]{1,0:T(8,128)S(1)}, f32[40,128]{1,0:T(8,128)S(1)}, f32[8,128]{1,0:T(8,128)S(1)}) custom-call(bf16[4,2,128,1024]{3,2,1,0:T(8,128)(2,1)} %bitcast.58, bf16[256,1024]{1,0:T(8,128)(2,1)S(1)} %convolution_convert_fusion.2.d_heads, bf16[1024,768]{1,0:T(8,128)(2,1)S(1)} %bitcast.57, ...), custom_call_target="tpu_custom_call" | custom-call | flops 20000000000 | bytes 25165824 | tf_op jit(solution)/shard_map/tail/pallas_call | solution.py:788
  344.4 1.9 copy-done.17
  346.2 15.3 %expert_grads.1 = (f32[4,1024,1024]{2,1,0:T(8,128)}, f32[4,1024,1024]{2,1,0:T(8,128)}) custom-call(bf16[4,384,1024]{2,1,0:T(8,128)(2,1)S(1)} %copy-done.14, bf16[4,384,1024]{2,1,0:T(8,128)(2,1)S(1)} %copy-done.17, bf16[4,384,1024]{2,1,0:T(8,128)(2,1)S(1)} %copy-done.16, bf16[4,384,1024]{2,1,0:T(8,128)(2,1)S(1)} %copy-done.15), custom_call_target="tpu_custom_call" | custom-call | flops 6442450944 | bytes 48234496 | tf_op jit(solution)/shard_map/expert_grads/pallas_call | solution.py:1100
  362.2 0.8 copy.56
  364.2 0.9 reshape.90
  365.6 1.8 convert_element_type.79
  367.4 1.0 copy.59
  (90 shorter events, 10.4 us)
Async XLA Ops:
  115.4 3.9 %copy-start = (bf16[256,1024]{1,0:T(8,128)(2,1)}, bf16[256,1024]{1,0:T(8,128)(2,1)S(1)}, u32[]{:S(2)}) copy-start(bf16[256,1024]{1,0:T(8,128)(2,1)S(1)} %get-tuple-element.40) | copy-start | bytes 1572868
  115.4 3.9 %copy-start.2 = (bf16[4,256,128]{2,1,0:T(8,128)(2,1)}, bf16[4,256,128]{2,1,0:T(8,128)(2,1)S(1)}, u32[]{:S(2)}) copy-start(bf16[4,256,128]{2,1,0:T(8,128)(2,1)S(1)} %get-tuple-element.43) | copy-start | bytes 786436
  115.5 3.9 %copy-start.11 = (bf16[4,256,768]{2,1,0:T(8,128)(2,1)}, bf16[4,256,768]{2,1,0:T(8,128)(2,1)S(1)}, u32[]{:S(2)}) copy-start(bf16[4,256,768]{2,1,0:T(8,128)(2,1)S(1)} %get-tuple-element.51) | copy-start | bytes 4718596
  115.5 3.9 %copy-start.18 = (bf16[1024,768]{1,0:T(8,128)(2,1)}, bf16[1024,768]{1,0:T(8,128)(2,1)S(1)}, u32[]{:S(2)}) copy-start(bf16[1024,768]{1,0:T(8,128)(2,1)S(1)} %get-tuple-element.54.qkv) | copy-start | bytes 4718596
  115.5 4.4 %copy-start.4 = (bf16[256,384]{1,0:T(8,128)(2,1)}, bf16[256,384]{1,0:T(8,128)(2,1)S(1)}, u32[]{:S(2)}) copy-start(bf16[256,384]{1,0:T(8,128)(2,1)S(1)} %get-tuple-element.44) | copy-start | bytes 589828
  119.4 1.8 copy-start.19
  119.9 1.3 copy-start.22
  121.2 152.3 %copy-start.28 = (s32[256]{0:T(256)S(1)}, s32[256]{0:T(256)}, u32[]{:S(2)}) copy-start(s32[256]{0:T(256)} %param.16) | copy-start | bytes 3076
  268.5 97.2 %collective-permute-start = (bf16[128,1024]{1,0:T(8,128)(2,1)}, bf16[128,1024]{1,0:T(8,128)(2,1)}, u32[]{:S(2)}, u32[]{:S(2)}) collective-permute-start(bf16[128,1024]{1,0:T(8,128)(2,1)} %get-tuple-element.59), channel_id=1, source_target_pairs={{0,0},{4,1},{8,2},{12,3},{16,4},{20,5},{24,6},{28,7},{1,8},{5,9},{... | collective-permute-start | bytes 786440 | tf_op jit(solution)/shard_map/ppermute | solution.py:1303
  273.6 3.7 %copy-start.3 = (bf16[4,256,128]{2,1,0:T(8,128)(2,1)S(1)}, bf16[4,256,128]{2,1,0:T(8,128)(2,1)}, u32[]{:S(2)}) copy-start(bf16[4,256,128]{2,1,0:T(8,128)(2,1)} %copy-done.2) | copy-start | bytes 786436
  273.6 3.7 %copy-start.26 = (f32[2,256,1024]{2,1,0:T(8,128)S(1)}, f32[2,256,1024]{2,1,0:T(8,128)}, u32[]{:S(2)}) copy-start(f32[2,256,1024]{2,1,0:T(8,128)} %get-tuple-element.48) | copy-start | bytes 6291460
  277.2 1.2 copy-start.5
  277.2 1.4 copy-start.20
  277.2 1.7 copy-start.25
  278.4 1.2 copy-start.7
  279.5 1.6 copy-start.21
  282.2 2.1 copy-start.27
  282.2 3.0 copy-start.9
  285.2 1.4 copy-start.12
  286.6 57.8 %copy-start.14 = (bf16[4,384,1024]{2,1,0:T(8,128)(2,1)S(1)}, bf16[4,384,1024]{2,1,0:T(8,128)(2,1)}, u32[]{:S(2)}) copy-start(bf16[4,384,1024]{2,1,0:T(8,128)(2,1)} %get-tuple-element.62.rows) | copy-start | bytes 9437188
  286.6 57.8 %copy-start.15 = (bf16[4,384,1024]{2,1,0:T(8,128)(2,1)S(1)}, bf16[4,384,1024]{2,1,0:T(8,128)(2,1)}, u32[]{:S(2)}) copy-start(bf16[4,384,1024]{2,1,0:T(8,128)(2,1)} %get-tuple-element.65.d_rows) | copy-start | bytes 9437188
  286.6 57.8 %copy-start.16 = (bf16[4,384,1024]{2,1,0:T(8,128)(2,1)S(1)}, bf16[4,384,1024]{2,1,0:T(8,128)(2,1)}, u32[]{:S(2)}) copy-start(bf16[4,384,1024]{2,1,0:T(8,128)(2,1)} %get-tuple-element.64.act) | copy-start | bytes 9437188
  344.4 1.9 copy-start.17
  346.2 15.9 %copy-start.24 = (f32[4,4,8,1024]{3,2,1,0:T(8,128)S(1)}, f32[4,4,8,1024]{3,2,1,0:T(8,128)}, u32[]{:S(2)}) copy-start(f32[4,4,8,1024]{3,2,1,0:T(8,128)} %convert_bitcast_fusion) | copy-start | bytes 1572868
  (6 other events, 6.1 us)
where the time goes:
time: 370 us; the launch traced here: 369 us
  Pallas kernels  327 us (88%)
  local copies, waits for them, and re-layouts  17.9 us (5%)
  matrix products  14.1 us (4%)
  other arithmetic  5.89 us (2%)
    pallas_call x1, Pallas kernels, middle(): pl.pallas_call(functools.partial(middle_kernel, (n_expert, groups, here,...  147 us
    pallas_call x1, Pallas kernels, head(): pl.pallas_call(functools.partial(head_kernel, (heads, HD ** (-0.5), group...  107 us
    pallas_call x1, Pallas kernels, tail(): pl.pallas_call(functools.partial(tail_kernel, heads, HD ** (-0.5)), name=...  57 us
    pallas_call x1, Pallas kernels, expert_grads(): pl.pallas_call(expert_grads_kernel, name='expert_grads', grid=(here, widt...  15.3 us
    unnamed x61, local copies, waits for them, and re-layouts  12.1 us
    dot_general x4, matrix products, mm(): return jnp.dot(left, right, preferred_element_type=F32)  9.48 us
  transfers between devices with their start and end apart: 1, of which 0 were waited for; matrix products, arithmetic and copies ran while one was open for 4% of the time, Pallas kernels for 20%

commit v1 on v0

--- a/solution.py
+++ b/solution.py
@@ -822,7 +822,7 @@
     sizes, source, gains, small, info, sort, w_qkv, w_attn, w_in, cotangent,
     normed, qkv, joined, lse, head_out, attn_full, in_here, small_full, grad_all, grad_rows, placer, gains_all,
     src_v, qkv_v, norm_v, join_v, acc, heads_low, attn_v, in_v, cot_v, slots, zbuf, row_v,
-    load_sem, store_sem, cut_sem, twin_sem, z_sem,
+    load_sem, store_sem, cut_sem, twin_sem, z_sem, level_sem,
 ):
     heads, scaling, groups, here, slab = sizes
     me, cut = lax.axis_index("expert"), lax.axis_index("cuts")
@@ -831,7 +831,8 @@
     at = [jnp.bitwise_xor(cut, k) for k in range(4)]
     n_cuts, tokens, width = src_v.shape
     n_expert, block = zbuf.shape[1], zbuf.shape[2]
-    own, half, part = width // n_cuts, tokens // 2, tokens // 4
+    own, half, levels = width // n_cuts, tokens // 2, n_expert // 2
+    level, quarter = lax.div(me, 2), tokens // n_expert
 
     def span(start, size, step):
         return pl.ds(pl.multiple_of(start, step), size)
@@ -886,11 +887,18 @@
 
         return view
 
-    def attn_view(owner, piece=None):
-        start = owner * tokens + core * half
-        if piece is None:
-            return attn_full.at[span(start, half, half)]
-        return attn_full.at[span(start + piece * part, part, part)]
+    def weight_rows(owner):
+        return span(owner * tokens + core * half + level * quarter, quarter, quarter)
+
+    def pass_levels(ref, base):
+        copies = []
+        for k in range(1, n_cuts):
+            view = ref.at[weight_rows(at[k])]
+            for n in range(1, levels):
+                peer = (2 * jnp.bitwise_xor(level, n) + core, cut)
+                copies.append(remote(view, view, level_sem, base + (k - 1) * (levels - 1) + n - 1, peer))
+                copies[-1].start()
+        return copies
 
     def slab_view(owner, piece=None):
         if piece is None:
@@ -906,19 +914,19 @@
     qkv_moved = []
     for n in range(3):
         qkv_moved += to_cuts(
-            lambda peer: w_qkv.at[span(core * half, half, half), span(n * width + peer * own, own, own)],
-            lambda k: qkv_v.at[span(cut * tokens + core * half, half, half), pl.ds(n * own, own)],
+            lambda peer: w_qkv.at[weight_rows(0), span(n * width + peer * own, own, own)],
+            lambda k: qkv_v.at[weight_rows(cut), pl.ds(n * own, own)],
             22 + 3 * n,
         )
-    for copy in gains_moved + tokens_moved[:2] + qkv_moved + small_moved:
-        copy.start()
     grad_moved = gather(whole(grad_all), cot_v, 4)
-    attn_moved = gather(attn_view, attn_v.at[span(core * half, half, half)], 8)
+    attn_moved = to_cuts(lambda peer: w_attn.at[weight_rows(0)], lambda k: attn_full.at[weight_rows(cut)], 8)
     slab_moved = gather(slab_view, row_v, 12)
     in_moved = to_cuts(
-        lambda peer: w_in.at[span(core * half, half, half), span(peer * width, width, width)],
-        lambda k: in_here.at[span(cut * tokens + core * half, half, half)], 31,
+        lambda peer: w_in.at[weight_rows(0), span(peer * width, width, width)],
+        lambda k: in_here.at[weight_rows(cut)], 31,
     )
+    for copy in gains_moved + tokens_moved[:2] + qkv_moved + attn_moved + in_moved + small_moved:
+        copy.start()
     head_moved = to_cuts(
         lambda peer: heads_low.at[span(peer * tokens, tokens, tokens)],
         lambda k: head_out.at[:, span(cut * own, own, own)], 34,
@@ -945,6 +953,11 @@
     gains_all[cut] = gains[...]
     small_full[cut] = small[...]
     relay(tokens_moved)
+    for copy in grad_moved[:2]:
+        copy.start()
+    for copy in qkv_moved:
+        copy.wait_recv()
+    qkv_levels = pass_levels(qkv_v, 0)
     for copy in loads[1:] + own_qkv:
         copy.wait()
     stores = [
@@ -964,7 +977,11 @@
     normalize(cut)
     normalize(at[1])
     normalize(at[2])
-    for copy in qkv_moved:
+    for copy in attn_moved + in_moved:
+        copy.wait_recv()
+    attn_levels = pass_levels(attn_full, 3 * (levels - 1))
+    in_levels = pass_levels(in_here, 6 * (levels - 1))
+    for copy in qkv_levels:
         copy.wait_recv()
 
     def share(ref, base):
@@ -978,8 +995,6 @@
     shared = share(qkv_v, 0)
     for copy in tokens_moved[2:]:
         copy.wait_recv()
-    for copy in grad_moved[:2] + attn_moved[:2] + in_moved:
-        copy.start()
     normalize(at[3])
     for copy in shared:
         copy.wait_recv()
@@ -999,6 +1014,8 @@
         flat = zbuf[g].reshape(n_expert * block, width)
         for j in range(per_group):
             row_v[g * per_group + j] = mm(sort[pl.ds(j * slab, slab), :], flat).astype(BF)
+    for copy in slab_moved[:2]:
+        copy.start()
     stores.append(local(row_v, slab_view(cut), store_sem, 6))
 
     @pl.loop(0, heads)
@@ -1006,9 +1023,6 @@
         @pl.when(head == 2)
         def _():
             relay(grad_moved)
-            relay(attn_moved)
-            for copy in slab_moved[:2]:
-                copy.start()
 
         pair = lax.div(head, 2)
         lane = lax.broadcasted_iota(jnp.int32, (1, 128), 1)
@@ -1037,18 +1051,17 @@
     for copy in head_moved:
         copy.start()
     head_out[:, span(cut * own, own, own)] = heads_low[span(cut * tokens, tokens, tokens), :]
-    for copy in in_moved:
-        copy.wait_recv()
-    shared += share(in_here, 3)
-    for copy in attn_moved[2:]:
-        copy.wait_recv()
-    shared += share(attn_full, 6)
     relay(slab_moved)
+    for copy in attn_levels + in_levels:
+        copy.wait_recv()
+    shared += share(attn_full, 3)
+    shared += share(in_here, 6)
     for copy in shared[3:] + grad_moved[2:] + slab_moved[2:] + head_moved + small_moved:
         copy.wait_recv()
     for copy in stores:
         copy.wait()
     everything = tokens_moved + gains_moved + small_moved + qkv_moved + grad_moved + attn_moved + slab_moved
+    everything += qkv_levels + attn_levels + in_levels
     for copy in everything + in_moved + head_moved + z_moved + shared:
         copy.wait_send()
 
@@ -1079,7 +1092,7 @@
             vmem((tokens, features), BF), vmem((tokens, features), BF), vmem((tokens, features), BF),
             vmem((groups, n_expert, block, features), BF), vmem((groups, n_expert, block, features), BF),
             vmem((here, slab, features), BF),
-            dma((6,)), dma((7,)), dma((2, 37)), dma((2, 9)), dma((2, groups * n_expert)),
+            dma((6,)), dma((7,)), dma((2, 37)), dma((2, 9)), dma((2, groups * n_expert)), dma((2, 9 * (n_expert // 2 - 1))),
         ],
         compiler_params=pltpu.CompilerParams(
             collective_id=3, has_side_effects=True, vmem_limit_bytes=48 << 20

time: 370 us -> 359 us (0.970)
  Pallas kernels: 327 us -> 315 us
    pallas_call x1, Pallas kernels: 107 us -> 89.7 us  [head(): pl.pallas_call(functools.partial(head_kernel, (heads, HD ** (-0.5), group...]
    pallas_call x1, Pallas kernels: 147 us -> 152 us  [middle(): pl.pallas_call(functools.partial(middle_kernel, (n_expert, groups, here,...]
  transfers between devices with their start and end apart: 1 -> 1, of which waited for: 0 -> 0; matrix products, arithmetic and copies ran while one was open for 4% -> 4% of each run, Pallas kernels for 20% -> 21%
where the time goes in v1:
time: 359 us; the launch traced here: 358 us
  Pallas kernels  315 us (88%)
  local copies, waits for them, and re-layouts  17.9 us (5%)
  matrix products  14.1 us (4%)
  other arithmetic  5.89 us (2%)
  starting transfers between devices  3.59 us (1%)
    pallas_call x1, Pallas kernels, middle(): pl.pallas_call(functools.partial(middle_kernel, (n_expert, groups, here,...  152 us
    pallas_call x1, Pallas kernels, head(): pl.pallas_call(functools.partial(head_kernel, (heads, HD ** (-0.5), group...  89.7 us
    pallas_call x1, Pallas kernels, tail(): pl.pallas_call(functools.partial(tail_kernel, heads, HD ** (-0.5)), name=...  58.1 us
    pallas_call x1, Pallas kernels, expert_grads(): pl.pallas_call(expert_grads_kernel, name='expert_grads', grid=(here, widt...  15.3 us
    unnamed x61, local copies, waits for them, and re-layouts  12.1 us
    dot_general x4, matrix products, mm(): return jnp.dot(left, right, preferred_element_type=F32)  9.48 us
  transfers between devices with their start and end apart: 1, of which 0 were waited for; matrix products, arithmetic and copies ran while one was open for 4% of the time, Pallas kernels for 21%

profile of v1, /device:TPU:0, one launch (start us, length us, event | category | flops | bytes accessed | tf_op | source)
XLA Modules:
  0.0 357.9 jit_solution(5211685156743365471)
XLA Ops:
  2.7 0.7 pad_maximum_fusion
  4.4 1.0 copy-done.6
  5.5 1.0 copy-done.8
  6.5 1.0 copy-done.10
  7.6 0.9 copy-done.13
  8.4 89.7 %head.1 = (bf16[4,256,1024]{2,1,0:T(8,128)(2,1)}, bf16[1024,768]{1,0:T(8,128)(2,1)S(1)}, bf16[4,256,768]{2,1,0:T(8,128)(2,1)S(1)}, f32[4,1,1024]{2,1,0:T(1,128)S...) custom-call(bf16[256,1024]{1,0:T(8,128)(2,1)S(1)} %copy-done.8, ...), custom_call_target="tpu_custom_call" | custom-call | flops 8000000000 | bytes 25165824 | tf_op jit(solution)/shard_map/head/pallas_call | solution.py:1077
  98.2 3.8 %fusion.26 = (f32[256]{0:T(256)S(1)}, f32[256,1024]{1,0:T(8,128)S(1)}) fusion(bf16[256,1024]{1,0:T(8,128)(2,1)S(1)} %get-tuple-element.40, bf16[1024,1024]{1,0:T(8,128)(2,1)} %get-tuple-element.41, bf16[256,1024]{1,0:T(8,128)(2,1)S(1)} %copy-done.8), kind=kOutput, calls=%fused_computation.80 | convolution fusion | flops 537657088 | bytes 4195328 | tf_op jit(solution)/shard_map/dot_general | solution.py:33
  102.6 1.3 convolution_convert_fusion.1
  103.9 152.3 %middle.1 = (f32[2,256,1024]{2,1,0:T(8,128)}, bf16[2,8,24,1024]{3,2,1,0:T(8,128)(2,1)}, bf16[2,8,24,1024]{3,2,1,0:T(8,128)(2,1)}, bf16[4,32,1024]{2,1,0:T(8,128)...) custom-call(bf16[2,8,24,1024]{3,2,1,0:T(8,128)(2,1)} %bitcast.61, ...), custom_call_target="tpu_custom_call" | custom-call | flops 21474836480 | bytes 50331648 | tf_op jit(solution)/shard_map/middle/pallas_call | solution.py:521
  256.2 3.6 %collective-permute-start = (bf16[128,1024]{1,0:T(8,128)(2,1)}, bf16[128,1024]{1,0:T(8,128)(2,1)}, u32[]{:S(2)}, u32[]{:S(2)}) collective-permute-start(bf16[128,1024]{1,0:T(8,128)(2,1)} %get-tuple-element.59), channel_id=1, source_target_pairs={{0,0},{4,1},{8,2},{12,3},{16,4},{20,5},{24,6},{28,7},{1,8},{5,9},{... | collective-permute-start | bytes 786440 | tf_op jit(solution)/shard_map/ppermute | solution.py:1316
  259.8 1.4 fusion.10
  261.3 3.6 fusion.1
  267.7 1.1 copy-done.21
  268.9 0.8 convolution_convert_fusion.2.d_heads
  269.9 2.1 convolution_convert_fusion
  272.0 0.8 convert_bitcast_fusion
  272.9 1.4 copy-done.12
  274.3 58.1 %tail.1 = (f32[256,1024]{1,0:T(8,128)S(1)}, bf16[4,32,768]{2,1,0:T(8,128)(2,1)S(1)}, f32[32,1024]{1,0:T(8,128)S(1)}, f32[40,128]{1,0:T(8,128)S(1)}, f32[8,128]{1,0:T(8,128)S(1)}) custom-call(bf16[4,2,128,1024]{3,2,1,0:T(8,128)(2,1)} %bitcast.58, bf16[256,1024]{1,0:T(8,128)(2,1)S(1)} %convolution_convert_fusion.2.d_heads, bf16[1024,768]{1,0:T(8,128)(2,1)S(1)} %bitcast.57, ...), custom_call_target="tpu_custom_call" | custom-call | flops 20000000000 | bytes 25165824 | tf_op jit(solution)/shard_map/tail/pallas_call | solution.py:788
  333.2 1.9 copy-done.17
  335.1 15.3 %expert_grads.1 = (f32[4,1024,1024]{2,1,0:T(8,128)}, f32[4,1024,1024]{2,1,0:T(8,128)}) custom-call(bf16[4,384,1024]{2,1,0:T(8,128)(2,1)S(1)} %copy-done.14, bf16[4,384,1024]{2,1,0:T(8,128)(2,1)S(1)} %copy-done.17, bf16[4,384,1024]{2,1,0:T(8,128)(2,1)S(1)} %copy-done.16, bf16[4,384,1024]{2,1,0:T(8,128)(2,1)S(1)} %copy-done.15), custom_call_target="tpu_custom_call" | custom-call | flops 6442450944 | bytes 48234496 | tf_op jit(solution)/shard_map/expert_grads/pallas_call | solution.py:1113
  351.0 0.8 copy.56
  353.0 0.9 reshape.90
  354.5 1.8 convert_element_type.79
  356.3 1.0 copy.59
  (90 shorter events, 10.4 us)
Async XLA Ops:
  98.1 3.9 %copy-start = (bf16[256,1024]{1,0:T(8,128)(2,1)}, bf16[256,1024]{1,0:T(8,128)(2,1)S(1)}, u32[]{:S(2)}) copy-start(bf16[256,1024]{1,0:T(8,128)(2,1)S(1)} %get-tuple-element.40) | copy-start | bytes 1572868
  98.1 3.9 %copy-start.2 = (bf16[4,256,128]{2,1,0:T(8,128)(2,1)}, bf16[4,256,128]{2,1,0:T(8,128)(2,1)S(1)}, u32[]{:S(2)}) copy-start(bf16[4,256,128]{2,1,0:T(8,128)(2,1)S(1)} %get-tuple-element.43) | copy-start | bytes 786436
  98.2 3.9 %copy-start.11 = (bf16[4,256,768]{2,1,0:T(8,128)(2,1)}, bf16[4,256,768]{2,1,0:T(8,128)(2,1)S(1)}, u32[]{:S(2)}) copy-start(bf16[4,256,768]{2,1,0:T(8,128)(2,1)S(1)} %get-tuple-element.51) | copy-start | bytes 4718596
  98.2 3.9 %copy-start.18 = (bf16[1024,768]{1,0:T(8,128)(2,1)}, bf16[1024,768]{1,0:T(8,128)(2,1)S(1)}, u32[]{:S(2)}) copy-start(bf16[1024,768]{1,0:T(8,128)(2,1)S(1)} %get-tuple-element.54.qkv) | copy-start | bytes 4718596
  98.2 4.4 %copy-start.4 = (bf16[256,384]{1,0:T(8,128)(2,1)}, bf16[256,384]{1,0:T(8,128)(2,1)S(1)}, u32[]{:S(2)}) copy-start(bf16[256,384]{1,0:T(8,128)(2,1)S(1)} %get-tuple-element.44) | copy-start | bytes 589828
  102.1 1.8 copy-start.19
  102.6 1.3 copy-start.22
  103.9 157.3 %copy-start.28 = (s32[256]{0:T(256)S(1)}, s32[256]{0:T(256)}, u32[]{:S(2)}) copy-start(s32[256]{0:T(256)} %param.16) | copy-start | bytes 3076
  256.2 98.3 %collective-permute-start = (bf16[128,1024]{1,0:T(8,128)(2,1)}, bf16[128,1024]{1,0:T(8,128)(2,1)}, u32[]{:S(2)}, u32[]{:S(2)}) collective-permute-start(bf16[128,1024]{1,0:T(8,128)(2,1)} %get-tuple-element.59), channel_id=1, source_target_pairs={{0,0},{4,1},{8,2},{12,3},{16,4},{20,5},{24,6},{28,7},{1,8},{5,9},{... | collective-permute-start | bytes 786440 | tf_op jit(solution)/shard_map/ppermute | solution.py:1316
  261.3 3.7 %copy-start.3 = (bf16[4,256,128]{2,1,0:T(8,128)(2,1)S(1)}, bf16[4,256,128]{2,1,0:T(8,128)(2,1)}, u32[]{:S(2)}) copy-start(bf16[4,256,128]{2,1,0:T(8,128)(2,1)} %copy-done.2) | copy-start | bytes 786436
  261.3 3.7 %copy-start.26 = (f32[2,256,1024]{2,1,0:T(8,128)S(1)}, f32[2,256,1024]{2,1,0:T(8,128)}, u32[]{:S(2)}) copy-start(f32[2,256,1024]{2,1,0:T(8,128)} %get-tuple-element.48) | copy-start | bytes 6291460
  264.9 1.2 copy-start.5
  264.9 1.4 copy-start.20
  264.9 1.7 copy-start.25
  266.1 1.2 copy-start.7
  267.3 1.6 copy-start.21
  269.9 2.1 copy-start.27
  269.9 3.0 copy-start.9
  272.9 1.4 copy-start.12
  274.3 58.9 %copy-start.14 = (bf16[4,384,1024]{2,1,0:T(8,128)(2,1)S(1)}, bf16[4,384,1024]{2,1,0:T(8,128)(2,1)}, u32[]{:S(2)}) copy-start(bf16[4,384,1024]{2,1,0:T(8,128)(2,1)} %get-tuple-element.62.rows) | copy-start | bytes 9437188
  274.3 58.9 %copy-start.15 = (bf16[4,384,1024]{2,1,0:T(8,128)(2,1)S(1)}, bf16[4,384,1024]{2,1,0:T(8,128)(2,1)}, u32[]{:S(2)}) copy-start(bf16[4,384,1024]{2,1,0:T(8,128)(2,1)} %get-tuple-element.65.d_rows) | copy-start | bytes 9437188
  274.3 58.9 %copy-start.16 = (bf16[4,384,1024]{2,1,0:T(8,128)(2,1)S(1)}, bf16[4,384,1024]{2,1,0:T(8,128)(2,1)}, u32[]{:S(2)}) copy-start(bf16[4,384,1024]{2,1,0:T(8,128)(2,1)} %get-tuple-element.64.act) | copy-start | bytes 9437188
  333.2 1.9 copy-start.17
  335.1 15.9 %copy-start.24 = (f32[4,4,8,1024]{3,2,1,0:T(8,128)S(1)}, f32[4,4,8,1024]{3,2,1,0:T(8,128)}, u32[]{:S(2)}) copy-start(f32[4,4,8,1024]{3,2,1,0:T(8,128)} %convert_bitcast_fusion) | copy-start | bytes 1572868
  (6 other events, 6.1 us)

commit v2 on v1

--- a/solution.py
+++ b/solution.py
@@ -675,12 +675,23 @@
     dj[:, pl.ds(2 * width, width)] = acc_v[...].astype(BF)
     for copy in later:
         copy.wait()
-    dn_moved = []
-    for k in (3, 1, 2):
+    part = tokens // 2
+    first, last = pl.ds(0, part), pl.ds(part, part)
+    at_x, at_y = (me, jnp.bitwise_xor(cut, 1)), (me, jnp.bitwise_xor(cut, 2))
+
+    def partial_sum(k):
         peer = jnp.bitwise_xor(cut, k)
         dn[k] = mm_nt(dj[columns(peer, tokens), :], qkv_v[...]).astype(BF)
-        dn_moved.append(send(dn.at[k], dn_in.at[k - 1], cut_sem, 6 + k - 1, (me, peer)))
-    sent.extend(dn_moved)
+
+    partial_sum(3)
+    passing = [
+        send(dn.at[3, first], dn_in.at[2, first], cut_sem, 6, at_x),
+        send(dn.at[3, last], dn_in.at[2, last], cut_sem, 7, at_y),
+    ]
+    partial_sum(1)
+    dn_moved = [send(dn.at[1, first], dn_in.at[0, first], cut_sem, 8, at_x)]
+    partial_sum(2)
+    dn_moved.append(send(dn.at[2, last], dn_in.at[1, last], cut_sem, 12, at_y))
 
     @pl.loop(0, levels)
     def _(step):
@@ -689,6 +700,12 @@
 
     twins.append(send(gq.at[:, other], core_q, core_sem, 1, twin))
     d_normed = mm_nt(dj[columns(cut, tokens), :], qkv_v[...])
+
+    for n, rows, k, index, peer in ((0, first, 2, 13, at_y), (1, last, 1, 14, at_x)):
+        passing[n].wait_recv()
+        dn[k, rows] = (dn[k, rows].astype(F32) + dn_in[2, rows].astype(F32)).astype(BF)
+        dn_moved.append(send(dn.at[k, rows], dn_in.at[k - 1, rows], cut_sem, index, peer))
+    sent.extend(passing + dn_moved)
 
     for copy in attn_moved:
         copy.wait_recv()
@@ -724,8 +741,7 @@
 
     for copy in dn_moved:
         copy.wait_recv()
-    for k in range(1, n_cuts):
-        d_normed = d_normed + dn_in[k - 1].astype(F32)
+    d_normed = d_normed + dn_in[0].astype(F32) + dn_in[1].astype(F32)
     xhat, inv = norm_parts(source[...].astype(F32))
     q = d_normed * gain[...]
     mean_q = jnp.mean(q, axis=-1, keepdims=True)
@@ -805,7 +821,7 @@
             vmem((seq_len, features), BF), vmem((features, wide), BF),
             vmem((n_expert, rows, 128), F32), vmem((rows, 128), F32), vmem((n_cuts, rows, 128), F32),
             vmem((8, features), F32), vmem((n_expert, 8, 128), F32), vmem((8, 128), F32), vmem((n_cuts, 8, 128), F32),
-            dma((3,)), dma((2, 2)), dma((2, 2 * (levels - 1))), dma((2, 4 * (n_cuts - 1))),
+            dma((3,)), dma((2, 2)), dma((2, 2 * (levels - 1))), dma((2, 15)),
             dma((2, 2 * (n_expert - 1))), dma((2, 2 * (n_cuts - 1))),
         ],
         compiler_params=pltpu.CompilerParams(
@@ -1101,28 +1117,47 @@
     )(source, gains, small, info, sort, w_qkv, w_attn, w_in, cotangent)
 
 
-def expert_grads_kernel(rows, d_first, act, d_rows, grad_in, grad_out):
-    grad_in[0] = mm_tn(rows[0], d_first[0])
-    grad_out[0] = mm_tn(act[0], d_rows[0])
+def expert_grads_kernel(rows, d_first, act, d_rows, grad_in, grad_out, rows_v, first_v, act_v, d_rows_v, sems):
+    expert, tile = pl.program_id(0), pl.program_id(1)
+    pairs = ((rows, rows_v), (d_first, first_v), (act, act_v), (d_rows, d_rows_v))
+
+    def copies(index):
+        return [pltpu.make_async_copy(src.at[index], dst.at[index], sems.at[n, index]) for n, (src, dst) in enumerate(pairs)]
+
+    @pl.when(jnp.logical_and(expert == 0, tile == 0))
+    def _():
+        for index in range(rows.shape[0]):
+            for copy in copies(index):
+                copy.start()
+
+    @pl.when(tile == 0)
+    def _():
+        for copy in copies(expert):
+            copy.wait()
+
+    span = tile_of(tile, 512)
+    grad_in[0] = mm_tn(rows_v[expert, :, span], first_v[expert])
+    grad_out[0] = mm_tn(act_v[expert, :, span], d_rows_v[expert])
 
 
 def expert_grads(rows, d_first, act, d_rows):
     here, count, width = rows.shape
     hidden = act.shape[2]
-    part = pl.BlockSpec((1, count, 256), lambda e, t: (e, 0, t))
+    any_spec = pl.BlockSpec(memory_space=pl.ANY)
     return pl.pallas_call(
         expert_grads_kernel,
         name="expert_grads",
-        grid=(here, width // 256),
+        grid=(here, width // 512),
         out_shape=(jax.ShapeDtypeStruct((here, width, hidden), F32), jax.ShapeDtypeStruct((here, hidden, width), F32)),
-        in_specs=[
-            part, pl.BlockSpec((1, count, hidden), lambda e, t: (e, 0, 0)),
-            part, pl.BlockSpec((1, count, width), lambda e, t: (e, 0, 0)),
+        in_specs=[any_spec] * 4,
+        out_specs=(
+            pl.BlockSpec((1, 512, hidden), lambda e, t: (e, t, 0)), pl.BlockSpec((1, 512, width), lambda e, t: (e, t, 0)),
+        ),
+        scratch_shapes=[
+            pltpu.VMEM(rows.shape, BF), pltpu.VMEM(d_first.shape, BF), pltpu.VMEM(act.shape, BF), pltpu.VMEM(d_rows.shape, BF),
+            pltpu.SemaphoreType.DMA((4, here)),
         ],
-        out_specs=(
-            pl.BlockSpec((1, 256, hidden), lambda e, t: (e, t, 0)), pl.BlockSpec((1, 256, width), lambda e, t: (e, t, 0)),
-        ),
-        compiler_params=pltpu.CompilerParams(vmem_limit_bytes=32 << 20),
+        compiler_params=pltpu.CompilerParams(vmem_limit_bytes=66_000_000),
         cost_estimate=pl.CostEstimate(flops=4 * here * count * width * hidden, bytes_accessed=46 << 20, transcendentals=0),
     )(rows, d_first, act, d_rows)
 
@@ -1313,6 +1348,7 @@
         swap = [
             ((flat % n_expert) * n_cuts + flat // n_expert, flat) for flat in range(n_expert * n_cuts)
         ]
+        s_out, late = lax.optimization_barrier((s_out, late))
         s_out = lax.ppermute(s_out, ("expert", "cuts"), swap).astype(F32)
         s_in = s_in.swapaxes(0, 1).reshape(-1, w_in.shape[1]).astype(F32)
         s_qkv = s_qkv.reshape(n_cuts, -1, 3, own).transpose(1, 2, 0, 3).reshape(-1, 3 * features).astype(F32)

time: 359 us -> 355 us (0.989)
    unnamed x61 -> x71, local copies, waits for them, and re-layouts: 12.1 us -> 9.8 us
  transfers between devices with their start and end apart: 1 -> 1, of which waited for: 0 -> 0; matrix products, arithmetic and copies ran while one was open for 4% -> 1% of each run, Pallas kernels for 21% -> 4%
where the time goes in v2:
time: 355 us
  Pallas kernels  315 us (89%)
  local copies, waits for them, and re-layouts  16.1 us (5%)
  matrix products  13 us (4%)
  other arithmetic  5.68 us (2%)
  starting transfers between devices  3.58 us (1%)
    pallas_call x1, Pallas kernels, middle(): pl.pallas_call(functools.partial(middle_kernel, (n_expert, groups, here,...  152 us
    pallas_call x1, Pallas kernels, head(): pl.pallas_call(functools.partial(head_kernel, (heads, HD ** (-0.5), group...  89.7 us
    pallas_call x1, Pallas kernels, tail(): pl.pallas_call(functools.partial(tail_kernel, heads, HD ** (-0.5)), name=...  58.5 us
    pallas_call x1, Pallas kernels, expert_grads(): pl.pallas_call(expert_grads_kernel, name='expert_grads', grid=(here, widt...  14.8 us
    unnamed x71, local copies, waits for them, and re-layouts  9.8 us
    dot_general x4, matrix products, mm(): return jnp.dot(left, right, preferred_element_type=F32)  8.35 us
  transfers between devices with their start and end apart: 1, of which 0 were waited for; matrix products, arithmetic and copies ran while one was open for 1% of the time, Pallas kernels for 4%

profile of v2, /device:TPU:0, one launch (start us, length us, event | category | flops | bytes accessed | tf_op | source)
XLA Modules:
  0.0 354.7 jit_solution(13689559425628384771)
XLA Ops:
  2.0 0.7 fusion.20
  2.7 0.7 pad_maximum_fusion
  3.5 0.7 add_convert_fusion
  4.4 1.0 copy-done.8
  5.5 1.0 copy-done.10
  6.5 1.0 copy-done.12
  7.6 0.9 copy-done.15
  8.4 89.7 %head.1 = (bf16[4,256,1024]{2,1,0:T(8,128)(2,1)}, bf16[1024,768]{1,0:T(8,128)(2,1)S(1)}, bf16[4,256,768]{2,1,0:T(8,128)(2,1)S(1)}, f32[4,1,1024]{2,1,0:T(1,128)S...) custom-call(bf16[256,1024]{1,0:T(8,128)(2,1)S(1)} %copy-done.10, ...), custom_call_target="tpu_custom_call" | custom-call | flops 8000000000 | bytes 25165824 | tf_op jit(solution)/shard_map/head/pallas_call | solution.py:1093
  98.2 3.8 %fusion.26 = (f32[256]{0:T(256)S(1)}, f32[256,1024]{1,0:T(8,128)S(1)}) fusion(bf16[256,1024]{1,0:T(8,128)(2,1)S(1)} %get-tuple-element.42, bf16[1024,1024]{1,0:T(8,128)(2,1)} %get-tuple-element.43, bf16[256,1024]{1,0:T(8,128)(2,1)S(1)} %copy-done.10), kind=kOutput, calls=%fused_computation.80 | convolution fusion | flops 537657088 | bytes 4195328 | tf_op jit(solution)/shard_map/dot_general | solution.py:33
  104.2 1.3 convolution_convert_fusion.1
  105.5 152.2 %middle.1 = (f32[2,256,1024]{2,1,0:T(8,128)}, bf16[2,8,24,1024]{3,2,1,0:T(8,128)(2,1)}, bf16[2,8,24,1024]{3,2,1,0:T(8,128)(2,1)}, bf16[4,32,1024]{2,1,0:T(8,128)...) custom-call(bf16[2,8,24,1024]{3,2,1,0:T(8,128)(2,1)} %bitcast.61, ...), custom_call_target="tpu_custom_call" | custom-call | flops 21474836480 | bytes 50331648 | tf_op jit(solution)/shard_map/middle/pallas_call | solution.py:521
  257.8 3.6 %fusion.1 = (f32[256]{0:T(256)S(1)}, f32[256]{0:T(256)S(1)}, f32[256]{0:T(256)S(1)}, bf16[256,1024]{1,0:T(8,128)(2,1)}) fusion(bf16[256,1024]{1,0:T(8,128)(2,1)} %cotangent.1, f32[256]{0:T(256)} %bitcast.75, f32[256]{0:T(256)} %select_reduce_fusion, f32[2,256,1024]{2,1,0:T(8,128)} %get-tuple-element.50, f32[256,1024]{1,0:T(8,128)} %copy-done.17, ...), kind=kOutput, calls=%fused_computation.11 | convolution fusion | flops 204995840 | bytes 4134912 | tf_op jit(solution)/shard_map/dot_general | solution.py:33
  264.2 1.1 copy-done.19
  265.3 0.7 convolution_convert_fusion.2.d_heads
  266.4 2.1 convolution_convert_fusion
  268.5 58.5 %tail.1 = (f32[256,1024]{1,0:T(8,128)S(1)}, bf16[4,32,768]{2,1,0:T(8,128)(2,1)S(1)}, f32[32,1024]{1,0:T(8,128)S(1)}, f32[40,128]{1,0:T(8,128)S(1)}, f32[8,128]{1,0:T(8,128)S(1)}) custom-call(bf16[4,2,128,1024]{3,2,1,0:T(8,128)(2,1)} %bitcast.58, bf16[256,1024]{1,0:T(8,128)(2,1)S(1)} %convolution_convert_fusion.2.d_heads, bf16[1024,768]{1,0:T(8,128)(2,1)S(1)} %bitcast.57, ...), custom_call_target="tpu_custom_call" | custom-call | flops 20000000000 | bytes 25165824 | tf_op jit(solution)/shard_map/tail/pallas_call | solution.py:804
  327.0 1.0 copy-done.4
  328.0 3.6 %collective-permute-start = (bf16[128,1024]{1,0:T(8,128)(2,1)}, bf16[128,1024]{1,0:T(8,128)(2,1)}, u32[]{:S(2)}, u32[]{:S(2)}) collective-permute-start(bf16[128,1024]{1,0:T(8,128)(2,1)} %get-tuple-element.63), channel_id=1, source_target_pairs={{0,0},{4,1},{8,2},{12,3},{16,4},{20,5},{24,6},{28,7},{1,8},{5,9},{... | collective-permute-start | bytes 786440 | tf_op jit(solution)/shard_map/ppermute | solution.py:1352
  332.4 14.8 %expert_grads.1 = (f32[4,1024,1024]{2,1,0:T(8,128)}, f32[4,1024,1024]{2,1,0:T(8,128)}) custom-call(bf16[4,384,1024]{2,1,0:T(8,128)(2,1)} %get-tuple-element.66.rows, bf16[4,384,1024]{2,1,0:T(8,128)(2,1)} %get-tuple-element.67.d_first, bf16[4,384,1024]{2,1,0:T(8,128)(2,1)} %get-tuple-element.68.act, bf16[4,384,1024]{2,1,0:T(8,128)(2,1)} %get-tuple-element.69.d_rows), custom_call_target="tpu_custom_call" | custom-call | flops 6442450944 | bytes 48234496 | tf_op jit(solution)/shard_map/expert_grads/pallas_call | solution.py:1147
  347.8 0.8 copy.56
  348.6 0.7 copy.55
  349.8 0.9 reshape.90
  351.3 1.8 convert_element_type.79
  353.1 1.0 copy.59
  (100 shorter events, 9.8 us)
Async XLA Ops:
  98.1 3.9 %copy-start = (bf16[256,1024]{1,0:T(8,128)(2,1)}, bf16[256,1024]{1,0:T(8,128)(2,1)S(1)}, u32[]{:S(2)}) copy-start(bf16[256,1024]{1,0:T(8,128)(2,1)S(1)} %get-tuple-element.42) | copy-start | bytes 1572868
  98.1 3.9 %copy-start.13 = (bf16[4,256,768]{2,1,0:T(8,128)(2,1)}, bf16[4,256,768]{2,1,0:T(8,128)(2,1)S(1)}, u32[]{:S(2)}) copy-start(bf16[4,256,768]{2,1,0:T(8,128)(2,1)S(1)} %get-tuple-element.53) | copy-start | bytes 4718596
  98.1 3.9 %copy-start.16 = (bf16[1024,768]{1,0:T(8,128)(2,1)}, bf16[1024,768]{1,0:T(8,128)(2,1)S(1)}, u32[]{:S(2)}) copy-start(bf16[1024,768]{1,0:T(8,128)(2,1)S(1)} %get-tuple-element.56.qkv) | copy-start | bytes 4718596
  98.2 4.4 %copy-start.2 = (bf16[4,256,128]{2,1,0:T(8,128)(2,1)}, bf16[4,256,128]{2,1,0:T(8,128)(2,1)S(1)}, u32[]{:S(2)}) copy-start(bf16[4,256,128]{2,1,0:T(8,128)(2,1)S(1)} %get-tuple-element.45) | copy-start | bytes 786436
  98.2 6.0 %copy-start.6 = (bf16[256,384]{1,0:T(8,128)(2,1)}, bf16[256,384]{1,0:T(8,128)(2,1)S(1)}, u32[]{:S(2)}) copy-start(bf16[256,384]{1,0:T(8,128)(2,1)S(1)} %get-tuple-element.46) | copy-start | bytes 589828
  102.0 3.4 copy-start.17
  102.6 2.9 copy-start.20
  102.9 2.6 copy-start.22
  102.9 2.5 copy-start.29
  103.0 2.5 copy-start.31
  257.7 3.7 %copy-start.23 = (f32[256,34]{0,1:T(8,128)S(1)}, f32[256,34]{0,1:T(8,128)}, u32[]{:S(2)}) copy-start(f32[256,34]{0,1:T(8,128)} %copy-done.22) | copy-start | bytes 104452
  257.7 3.7 %copy-start.30 = (f32[256]{0:T(256)S(1)}, f32[256]{0:T(256)}, u32[]{:S(2)}) copy-start(f32[256]{0:T(256)} %copy-done.29) | copy-start | bytes 3076
  257.7 3.7 %copy-start.28 = (s32[256]{0:T(256)S(1)}, s32[256]{0:T(256)}, u32[]{:S(2)}) copy-start(s32[256]{0:T(256)} %param.16) | copy-start | bytes 3076
  257.8 3.7 %copy-start.32 = (f32[256]{0:T(256)S(1)}, f32[256]{0:T(256)}, u32[]{:S(2)}) copy-start(f32[256]{0:T(256)} %copy-done.31) | copy-start | bytes 3076
  257.8 3.7 %copy-start.33 = (f32[256]{0:T(256)S(1)}, f32[256]{0:T(256)}, u32[]{:S(2)}) copy-start(f32[256]{0:T(256)} %select_reduce_fusion) | copy-start | bytes 3076
  257.8 3.8 %copy-start.3 = (bf16[4,256,128]{2,1,0:T(8,128)(2,1)S(1)}, bf16[4,256,128]{2,1,0:T(8,128)(2,1)}, u32[]{:S(2)}) copy-start(bf16[4,256,128]{2,1,0:T(8,128)(2,1)} %copy-done.2) | copy-start | bytes 786436
  257.8 3.8 %copy-start.25 = (f32[2,256,1024]{2,1,0:T(8,128)S(1)}, f32[2,256,1024]{2,1,0:T(8,128)}, u32[]{:S(2)}) copy-start(f32[2,256,1024]{2,1,0:T(8,128)} %get-tuple-element.50) | copy-start | bytes 6291460
  261.4 1.7 copy-start.24
  263.7 1.6 copy-start.19
  266.4 2.1 copy-start.11
  266.4 2.1 copy-start.14
  268.5 63.1 %copy-start.26 = (bf16[4,32,1024]{2,1,0:T(8,128)(2,1)S(1)}, bf16[4,32,1024]{2,1,0:T(8,128)(2,1)}, u32[]{:S(2)}) copy-start(bf16[4,32,1024]{2,1,0:T(8,128)(2,1)} %get-tuple-element.60) | copy-start | bytes 786436
  328.0 23.3 %collective-permute-start = (bf16[128,1024]{1,0:T(8,128)(2,1)}, bf16[128,1024]{1,0:T(8,128)(2,1)}, u32[]{:S(2)}, u32[]{:S(2)}) collective-permute-start(bf16[128,1024]{1,0:T(8,128)(2,1)} %get-tuple-element.63), channel_id=1, source_target_pairs={{0,0},{4,1},{8,2},{12,3},{16,4},{20,5},{24,6},{28,7},{1,8},{5,9},{... | collective-permute-start | bytes 786440 | tf_op jit(solution)/shard_map/ppermute | solution.py:1352
  347.8 5.3 %copy-start.5 = (f32[256,1024]{1,0:T(8,128)S(1)}, f32[256,1024]{1,0:T(8,128)}, u32[]{:S(2)}) copy-start(f32[256,1024]{1,0:T(8,128)} %copy-done.4) | copy-start | bytes 3145732
  (11 other events, 11.9 us)

commit v3 on v2

--- a/solution.py
+++ b/solution.py
@@ -1111,7 +1111,7 @@
             dma((6,)), dma((7,)), dma((2, 37)), dma((2, 9)), dma((2, groups * n_expert)), dma((2, 9 * (n_expert // 2 - 1))),
         ],
         compiler_params=pltpu.CompilerParams(
-            collective_id=3, has_side_effects=True, vmem_limit_bytes=48 << 20
+            collective_id=3, has_side_effects=True, vmem_limit_bytes=66_000_000
         ),
         cost_estimate=pl.CostEstimate(flops=8_000_000_000, bytes_accessed=24 << 20, transcendentals=0),
     )(source, gains, small, info, sort, w_qkv, w_attn, w_in, cotangent)

time: 355 us -> 355 us (level)
    unnamed x71 -> x49, local copies, waits for them, and re-layouts: 9.8 us -> 6.9 us
where the time goes in v3:
time: 355 us; the launch traced here: 354 us
  Pallas kernels  317 us (89%)
  local copies, waits for them, and re-layouts  15.3 us (4%)
  matrix products  11.8 us (3%)
  other arithmetic  5.68 us (2%)
  starting transfers between devices  3.58 us (1%)
    pallas_call x1, Pallas kernels, middle(): pl.pallas_call(functools.partial(middle_kernel, (n_expert, groups, here,...  152 us
    pallas_call x1, Pallas kernels, head(): pl.pallas_call(functools.partial(head_kernel, (heads, HD ** (-0.5), group...  92 us
    pallas_call x1, Pallas kernels, tail(): pl.pallas_call(functools.partial(tail_kernel, heads, HD ** (-0.5)), name=...  58.4 us
    pallas_call x1, Pallas kernels, expert_grads(): pl.pallas_call(expert_grads_kernel, name='expert_grads', grid=(here, widt...  14.8 us
    dot_general x4, matrix products, mm(): return jnp.dot(left, right, preferred_element_type=F32)  7.12 us
  transfers between devices with their start and end apart: 1, of which 0 were waited for; matrix products, arithmetic and copies ran while one was open for 1% of the time, Pallas kernels for 4%

profile of v3, /device:TPU:0, one launch (start us, length us, event | category | flops | bytes accessed | tf_op | source)
XLA Modules:
  0.0 354.3 jit_solution(15158479110087657472)
XLA Ops:
  2.0 0.7 fusion.20
  2.7 0.7 pad_maximum_fusion
  3.5 0.7 add_convert_fusion
  4.2 0.8 copy.52.info
  6.3 92.0 %head.1 = (bf16[4,256,1024]{2,1,0:T(8,128)(2,1)}, bf16[1024,768]{1,0:T(8,128)(2,1)}, bf16[4,256,768]{2,1,0:T(8,128)(2,1)}, f32[4,1,1024]{2,1,0:T(1,128)}, bf16[2...) custom-call(bf16[256,1024]{1,0:T(8,128)(2,1)} %source.3, ...), custom_call_target="tpu_custom_call" | custom-call | flops 8000000000 | bytes 25165824 | tf_op jit(solution)/shard_map/head/pallas_call | solution.py:1093
  98.3 0.8 fusion.24
  99.2 2.6 fusion.26
  102.1 0.7 copy-done.6
  104.5 1.3 convolution_convert_fusion.1
  105.7 151.7 %middle.1 = (f32[2,256,1024]{2,1,0:T(8,128)}, bf16[2,8,24,1024]{3,2,1,0:T(8,128)(2,1)}, bf16[2,8,24,1024]{3,2,1,0:T(8,128)(2,1)}, bf16[4,32,1024]{2,1,0:T(8,128)...) custom-call(bf16[2,8,24,1024]{3,2,1,0:T(8,128)(2,1)} %bitcast.61, ...), custom_call_target="tpu_custom_call" | custom-call | flops 21474836480 | bytes 50331648 | tf_op jit(solution)/shard_map/middle/pallas_call | solution.py:521
  257.5 3.6 %fusion.1 = (f32[256]{0:T(256)S(1)}, f32[256]{0:T(256)S(1)}, f32[256]{0:T(256)S(1)}, bf16[256,1024]{1,0:T(8,128)(2,1)}) fusion(bf16[256,1024]{1,0:T(8,128)(2,1)} %cotangent.1, f32[256]{0:T(256)} %bitcast.75, f32[256]{0:T(256)S(1)} %select_reduce_fusion, f32[2,256,1024]{2,1,0:T(8,128)} %get-tuple-element.50, f32[256,1024]{1,0:T(8,128)} %copy-done.6, ...), kind=kOutput, calls=%fused_computation.11 | convolution fusion | flops 204995840 | bytes 4134912 | tf_op jit(solution)/shard_map/dot_general | solution.py:33
  262.7 0.7 multiply_reduce_fusion
  263.9 1.1 copy-done.8
  265.0 0.8 convolution_convert_fusion.2.d_heads
  266.1 2.1 convolution_convert_fusion
  268.2 58.4 %tail.1 = (f32[256,1024]{1,0:T(8,128)S(1)}, bf16[4,32,768]{2,1,0:T(8,128)(2,1)S(1)}, f32[32,1024]{1,0:T(8,128)S(1)}, f32[40,128]{1,0:T(8,128)S(1)}, f32[8,128]{1,0:T(8,128)S(1)}) custom-call(bf16[4,2,128,1024]{3,2,1,0:T(8,128)(2,1)} %bitcast.55, bf16[256,1024]{1,0:T(8,128)(2,1)S(1)} %convolution_convert_fusion.2.d_heads, bf16[1024,768]{1,0:T(8,128)(2,1)S(1)} %bitcast.54, ...), custom_call_target="tpu_custom_call" | custom-call | flops 20000000000 | bytes 25165824 | tf_op jit(solution)/shard_map/tail/pallas_call | solution.py:804
  326.7 1.0 copy-done
  327.6 3.6 %collective-permute-start = (bf16[128,1024]{1,0:T(8,128)(2,1)}, bf16[128,1024]{1,0:T(8,128)(2,1)}, u32[]{:S(2)}, u32[]{:S(2)}) collective-permute-start(bf16[128,1024]{1,0:T(8,128)(2,1)} %get-tuple-element.63), channel_id=1, source_target_pairs={{0,0},{4,1},{8,2},{12,3},{16,4},{20,5},{24,6},{28,7},{1,8},{5,9},{... | collective-permute-start | bytes 786440 | tf_op jit(solution)/shard_map/ppermute | solution.py:1352
  332.0 14.8 %expert_grads.1 = (f32[4,1024,1024]{2,1,0:T(8,128)}, f32[4,1024,1024]{2,1,0:T(8,128)}) custom-call(bf16[4,384,1024]{2,1,0:T(8,128)(2,1)} %get-tuple-element.66.rows, bf16[4,384,1024]{2,1,0:T(8,128)(2,1)} %get-tuple-element.67.d_first, bf16[4,384,1024]{2,1,0:T(8,128)(2,1)} %get-tuple-element.68.act, bf16[4,384,1024]{2,1,0:T(8,128)(2,1)} %get-tuple-element.69.d_rows), custom_call_target="tpu_custom_call" | custom-call | flops 6442450944 | bytes 48234496 | tf_op jit(solution)/shard_map/expert_grads/pallas_call | solution.py:1147
  347.4 0.8 copy.56
  348.3 0.7 copy.55
  349.4 0.9 reshape.90
  350.9 1.8 convert_element_type.79
  352.7 1.0 copy.59
  (78 shorter events, 10.0 us)
Async XLA Ops:
  6.3 92.9 %copy-start.2 = (bf16[256,1024]{1,0:T(8,128)(2,1)S(1)}, bf16[256,1024]{1,0:T(8,128)(2,1)}, u32[]{:S(2)}) copy-start(bf16[256,1024]{1,0:T(8,128)(2,1)} %source.3) | copy-start | bytes 1572868
  101.8 1.0 copy-start.6
  101.8 1.2 copy-start.12
  101.8 1.6 copy-start.22
  101.8 2.7 copy-start.16
  102.9 1.5 copy-start.9
  103.2 0.6 copy-start.14
  257.4 3.6 %copy-start.15 = (f32[256,34]{0,1:T(8,128)S(1)}, f32[256,34]{0,1:T(8,128)}, u32[]{:S(2)}) copy-start(f32[256,34]{0,1:T(8,128)} %copy-done.14) | copy-start | bytes 104452
  257.4 3.7 %copy-start.13 = (bf16[4,256,128]{2,1,0:T(8,128)(2,1)S(1)}, bf16[4,256,128]{2,1,0:T(8,128)(2,1)}, u32[]{:S(2)}) copy-start(bf16[4,256,128]{2,1,0:T(8,128)(2,1)} %get-tuple-element.45) | copy-start | bytes 786436
  257.5 3.7 %copy-start.20 = (f32[2,256,1024]{2,1,0:T(8,128)S(1)}, f32[2,256,1024]{2,1,0:T(8,128)}, u32[]{:S(2)}) copy-start(f32[2,256,1024]{2,1,0:T(8,128)} %get-tuple-element.50) | copy-start | bytes 6291460
  261.1 1.0 copy-start.10
  261.1 1.4 copy-start.7
  261.1 1.4 copy-start.17
  261.1 1.7 copy-start.18
  262.3 1.2 copy-start.19
  263.4 1.6 copy-start.8
  265.0 1.0 copy-start.11
  266.1 2.1 copy-start.3
  266.1 2.1 copy-start.4
  266.1 2.1 copy-start.5
  268.2 63.0 %copy-start.21 = (bf16[4,32,1024]{2,1,0:T(8,128)(2,1)S(1)}, bf16[4,32,1024]{2,1,0:T(8,128)(2,1)}, u32[]{:S(2)}) copy-start(bf16[4,32,1024]{2,1,0:T(8,128)(2,1)} %get-tuple-element.60) | copy-start | bytes 786436
  326.6 1.0 copy-start
  327.6 23.3 %collective-permute-start = (bf16[128,1024]{1,0:T(8,128)(2,1)}, bf16[128,1024]{1,0:T(8,128)(2,1)}, u32[]{:S(2)}, u32[]{:S(2)}) collective-permute-start(bf16[128,1024]{1,0:T(8,128)(2,1)} %get-tuple-element.63), channel_id=1, source_target_pairs={{0,0},{4,1},{8,2},{12,3},{16,4},{20,5},{24,6},{28,7},{1,8},{5,9},{... | collective-permute-start | bytes 786440 | tf_op jit(solution)/shard_map/ppermute | solution.py:1352
  347.4 5.3 %copy-start.1 = (f32[256,1024]{1,0:T(8,128)S(1)}, f32[256,1024]{1,0:T(8,128)}, u32[]{:S(2)}) copy-start(f32[256,1024]{1,0:T(8,128)} %copy-done) | copy-start | bytes 3145732
